TPU v7x, 128 devices: a whole 4x4x4 slice. The times are simulated.
128 devices in a mesh: lat: 16 (over x, y), lon: 4 (over z_lo, core), mem: 2 (over z_hi).
Axes of the slice: x: 4, y: 4, z: 4 (z_hi: 2, z_lo: 2; z = z_hi * 2 + z_lo), core: 2. Of those that a mesh axis runs over, the one named last changes fastest.
Arguments:
- velo: float32 [2, 4, 512, 2048], P(None, None, 'lat', 'lon'), may hold values from -6 to 6
- temp: float32 [4, 512, 2048], P(None, 'lat', 'lon'), may hold values from -6 to 6
- land: int32 [512, 2048], P('lat', 'lon'), may hold values 0 or 1
- target: bfloat16 [2, 4, 128, 512], P(None, None, 'lat', 'lon'), may hold values from -3 to 3
- w_first: bfloat16 [4, 9, 64, 3], P('mem'), may hold values from -1.25 to 1.25
- w_middle: bfloat16 [4, 9, 64, 64], P('mem'), may hold values from -0.25 to 0.25
- w_last: bfloat16 [4, 9, 2, 64], P('mem'), may hold values from -0.25 to 0.25
Outputs:
- velo_next: float32 [2, 4, 512, 2048], P(None, None, 'lat', 'lon')
- temp_next: float32 [4, 512, 2048], P(None, 'lat', 'lon')
- grad_first: float32 [4, 9, 64, 3], P('mem')
- grad_middle: float32 [4, 9, 64, 64], P('mem')
- grad_last: float32 [4, 9, 2, 64], P('mem')
All inputs are finite; a program needn't handle non-finite values. No bound on the sum of `land` on one device may be relied on, other than what follows from the above.
Results may differ from a plain program's by a relative error of at most 0.0003.
Values may be sent and summed in bfloat16 or wider, within the bound.
A program may use at most 128 MiB of HBM per device.

v0:
```python
import math

import jax
import jax.numpy as jnp
from jax import lax
from jax.sharding import PartitionSpec as P

LEV = 4
COARSE = 4


def with_halo(value, sides, width, wrap):
    for axis, dim in sides:
        size, length = (lax.axis_size(axis), value.shape[dim])
        up = [(i, (i + 1) % size) for i in range(size if wrap else size - 1)]
        down = [(j, i) for i, j in up]
        last = lax.slice_in_dim(value, length - width, length, axis=dim)
        first = lax.slice_in_dim(value, 0, width, axis=dim)
        before = lax.ppermute(last, axis, up)
        after = lax.ppermute(first, axis, down)
        value = jnp.concatenate([before, value, after], axis=dim)
    return value


def pad_cols(values):
    values = jnp.concatenate([values[..., -1:], values, values[..., :1]], axis=4)
    return values


def pad_act(values):
    values = with_halo(values, (("lat", 3),), 1, False)
    return pad_cols(values)


def conv_sum(padded, weights, form, sign):
    height = padded.shape[-2] - 2
    width = padded.shape[-1] - 2
    total = None
    for a in (-1, 0, 1):
        for b in (-1, 0, 1):
            k = (a + 1) * 3 + (b + 1)
            piece = padded[
                ..., 1 + sign * a : 1 + sign * a + height, 1 + sign * b : 1 + sign * b + width
            ]
            term = jnp.einsum(form, weights[:, k], piece, preferred_element_type=jnp.float32)
            total = term if total is None else total + term
    return total


def weight_grad(cotangent, padded, form):
    height = cotangent.shape[-2]
    width = cotangent.shape[-1]
    result = []
    for a in (-1, 0, 1):
        for b in (-1, 0, 1):
            piece = padded[..., 1 + a : 1 + a + height, 1 + b : 1 + b + width]
            result.append(jnp.einsum(form, cotangent, piece, preferred_element_type=jnp.float32))
    return jnp.stack(result, 1)


def per_device(velo, temp, land, target, w_first, w_middle, w_last):
    fields = jnp.concatenate([velo, temp[None]], 0)
    rows = fields.shape[2]
    cols = fields.shape[3]
    coarse = (
        fields.reshape(3, LEV, rows // COARSE, COARSE, cols // COARSE, COARSE)
        .mean(axis=(3, 5))
        .astype(jnp.bfloat16)
    )
    count = (
        2.0
        * LEV
        * (rows // COARSE)
        * lax.axis_size("lat")
        * (cols // COARSE)
        * lax.axis_size("lon")
    )
    members = w_first.shape[0] * lax.axis_size("mem")
    inputs, goal = (
        lax.all_to_all(coarse, "lon", split_axis=1, concat_axis=3, tiled=True),
        lax.all_to_all(target, "lon", split_axis=1, concat_axis=3, tiled=True),
    )
    xpad = pad_act(inputs[None])[0]
    hidden_one = jnp.tanh(conv_sum(xpad, w_first, "moc,clyx->molyx", 1)).astype(jnp.bfloat16)
    hpad_one = pad_act(hidden_one)
    hidden_two = jnp.tanh(conv_sum(hpad_one, w_middle, "moc,mclyx->molyx", 1)).astype(jnp.bfloat16)
    hpad_two = pad_act(hidden_two)
    predict = conv_sum(hpad_two, w_last, "moc,mclyx->molyx", 1)
    cot_three = ((predict - goal.astype(jnp.float32)[None]) * (2.0 / count)).astype(jnp.bfloat16)
    grad_three = weight_grad(cot_three, hpad_two, "molyx,mclyx->moc")
    two_f = hidden_two.astype(jnp.float32)
    cot_two = (
        conv_sum(pad_act(cot_three), w_last, "moc,molyx->mclyx", -1) * (1.0 - two_f * two_f)
    ).astype(jnp.bfloat16)
    grad_two = weight_grad(cot_two, hpad_one, "molyx,mclyx->moc")
    one_f = hidden_one.astype(jnp.float32)
    cot_one = (
        conv_sum(pad_act(cot_two), w_middle, "moc,molyx->mclyx", -1) * (1.0 - one_f * one_f)
    ).astype(jnp.bfloat16)
    grad_one = weight_grad(cot_one, xpad, "molyx,clyx->moc")
    summed = lax.psum(jnp.sum(predict, 0).astype(jnp.bfloat16), "mem").astype(jnp.float32)
    mean_force = summed / members
    mean_force = lax.all_to_all(
        mean_force.astype(jnp.bfloat16), "lon", split_axis=3, concat_axis=1, tiled=True
    ).astype(mean_force.dtype)
    force = jnp.repeat(jnp.repeat(mean_force, COARSE, axis=2), COARSE, axis=3)
    padded = with_halo(fields, (("lat", 2),), 1, False)
    padded = with_halo(padded, (("lon", 3),), 1, True)
    centre = padded[:, :, 1:-1, 1:-1]
    east = padded[:, :, 1:-1, 2:]
    west = padded[:, :, 1:-1, :-2]
    north = padded[:, :, 2:, 1:-1]
    south = padded[:, :, :-2, 1:-1]
    laplace = east + west + north + south - 4.0 * centre
    press = -jnp.cumsum(0.5 * padded[2], axis=0)
    grad_x = (press[:, 1:-1, 2:] - press[:, 1:-1, :-2]) / 2.0
    grad_y = (press[:, 2:, 1:-1] - press[:, :-2, 1:-1]) / 2.0
    total_rows = rows * lax.axis_size("lat")
    row_ids = (lax.axis_index("lat") * rows + jnp.arange(rows)).astype(jnp.float32)
    coriolis = jnp.sin(-math.pi / 2 + math.pi * (row_ids + 0.5) / total_rows)[:, None]
    wet = land.astype(jnp.float32)
    u_now = centre[0]
    v_now = centre[1]
    t_now = centre[2]
    u_next = u_now + 0.1 * wet * (coriolis * v_now - grad_x + 0.5 * laplace[0] + force[0])
    v_next = v_now + 0.1 * wet * (-coriolis * u_now - grad_y + 0.5 * laplace[1] + force[1])
    advect = u_now * (east[2] - west[2]) / 2.0 + v_now * (north[2] - south[2]) / 2.0
    t_next = t_now + 0.1 * wet * (-advect + 0.3 * laplace[2])
    grad_first, grad_middle, grad_last = lax.psum((grad_one, grad_two, grad_three), ("lat", "lon"))
    return (jnp.stack([u_next, v_next], 0), t_next, grad_first, grad_middle, grad_last)


def solution(mesh):
    return jax.shard_map(
        per_device,
        mesh=mesh,
        in_specs=(
            P(None, None, "lat", "lon"),
            P(None, "lat", "lon"),
            P("lat", "lon"),
            P(None, None, "lat", "lon"),
            P("mem", None, None, None),
            P("mem", None, None, None),
            P("mem", None, None, None),
        ),
        out_specs=(
            P(None, None, "lat", "lon"),
            P(None, "lat", "lon"),
            P("mem", None, None, None),
            P("mem", None, None, None),
            P("mem", None, None, None),
        ),
        check_vma=False,
    )
```

profile of v0, /device:TPU:1, one launch (start us, length us, event | category | flops | bytes accessed | tf_op | source)
XLA Modules:
  0.0 756.5 jit_solution(12206915258735823016)
XLA Ops:
  10.4 4.8 collective-permute-start
  15.1 10.9 %concatenate.122 = f32[1,4,8,4,128,4]{5,4,3,2,1,0:T(8,128)} reshape(f32[4,32,512]{2,1,0:T(8,128)} %param.8) | data formatting | bytes 524288 | tf_op jit(solution)/shard_map/concatenate | solution.py:62
  26.0 18.6 %concatenate.121 = f32[2,4,8,4,128,4]{5,4,3,2,1,0:T(8,128)} reshape(f32[2,4,32,512]{3,2,1,0:T(8,128)S(1)} %copy-done.19) | data formatting | bytes 1048576 | tf_op jit(solution)/shard_map/concatenate | solution.py:62
  44.6 5.2 copy.827
  49.9 10.0 %copy.826 = f32[2,4,8,4,128,4]{4,2,5,3,1,0:T(8,128)S(1)} copy(f32[2,4,8,4,128,4]{5,4,3,2,1,0:T(8,128)} %concatenate.121) | data formatting | bytes 1048576 | tf_op jit(solution)/shard_map/concatenate | solution.py:62
  60.6 4.6 all-to-all-start
  71.8 3.3 all-to-all-start.2
  75.1 3.2 collective-permute-start.4
  80.4 3.0 collective-permute-done.5
  90.6 5.5 collective-permute-start.6
  98.8 3.1 collective-permute-start.2
  115.5 3.1 fusion.115
  118.6 3.2 copy.1053
  121.8 3.1 copy.1052
  124.9 9.0 %fusion = f32[3,4,32,512]{2,3,1,0:T(8,128)S(1)} fusion(f32[3,4,1,512]{2,3,1,0:T(8,128)} %copy.822, f32[3,4,32,512]{2,3,1,0:T(8,128)} %copy.821, f32[3,4,1,512]{2,3,1,0:T(8,128)} %copy.823, f32[3,4,32,512]{2,3,1,0:T(8,128)} %copy.1052, f32[3,4,32,512]{2,3,1,0:T(8,128)} %copy.1053), kind=kLoop, calls=%fused_computation.1 | loop fusion | flops 1376256 | bytes 3194880 | tf_op jit(solution)/shard_map/sub | solution.py:114
  151.7 5.8 collective-permute-start.8
  171.8 10.0 %psum.28 = bf16[2,1,8,512]{3,2,1,0:T(8,128)(2,1)S(1)} all-reduce(bf16[2,1,8,512]{3,2,1,0:T(8,128)(2,1)S(1)} %bitcast.712), channel_id=1, replica_groups=mesh['lat'=16,'lon'=4,'mem'=2] {'mem'}, use_global_device_ids=true, to_apply=%region_3.0 | all-reduce | flops 8192 | bytes 32768 | tf_op jit(solution)/shard_map/psum | solution.py:101
  189.1 3.9 collective-permute-start.10
  195.4 6.6 all-to-all-start.1
  215.3 6.0 collective-permute-start.12
  244.2 4.1 fusion.80
  252.2 2.6 fusion.3
  268.4 274.7 %all-reduce = (f32[2,9,64,3]{2,3,0,1:T(4,128)S(1)}, f32[2,9,2,64]{3,2,0,1:T(2,128)S(1)}) all-reduce(f32[2,9,64,3]{2,3,0,1:T(4,128)S(1)} %fusion.19, f32[2,9,2,64]{3,2,0,1:T(2,128)S(1)} %copy-done.36), channel_id=1, replica_groups=mesh['lat'=16,'lon'=4,'mem'=2] {'lat','lon'}, use_global_device_ids=true, to_apply=%region_4.5 | all-reduce | flops 5760 | bytes 46080 | tf_op jit(solution)/shard_map/psum | solution.py:129
  544.4 203.1 %all-reduce.3.cloned.1.call-done = f32[2,9,64,64]{3,2,0,1:T(8,128)} async-done(((f32[2,9,64,64]{3,2,0,1:T(8,128)}), f32[2,9,64,64]{3,2,0,1:T(8,128)}) %all-reduce.3.cloned.1.call-update) | async-done | bytes 294928 | tf_op jit(solution)/shard_map/psum | solution.py:129
  (256 shorter events, 133.9 us)
Async XLA Ops:
  8.4 58.8 %copy-start.17 = (f32[3,4,32,512]{3,2,1,0:T(8,128)}, f32[3,4,32,512]{3,2,1,0:T(8,128)S(1)}, u32[]{:S(2)}) copy-start(f32[3,4,32,512]{3,2,1,0:T(8,128)S(1)} %pad_maximum_fusion.20) | copy-start | bytes 2359300
  8.4 89.5 %collective-permute-start.1 = (f32[3,4,1,512]{3,1,2,0:T(4,128)S(1)}, f32[3,4,1,512]{3,1,2,0:T(4,128)S(1)}, u32[]{:S(2)}, u32[]{:S(2)}) collective-permute-start(f32[3,4,1,512]{3,1,2,0:T(4,128)S(1)} %copy.1166), channel_id=1, source_target_pairs={{8,0},{16,8},{24,16},{32,24},{40,32},{48,40},{56,48},{64,56},{72,6... | collective-permute-start | bytes 73736 | tf_op jit(solution)/shard_map/ppermute | solution.py:20
  10.4 15.7 %copy-start.19 = (f32[2,4,32,512]{3,2,1,0:T(8,128)S(1)}, f32[2,4,32,512]{3,2,1,0:T(8,128)}, u32[]{:S(2)}) copy-start(f32[2,4,32,512]{3,2,1,0:T(8,128)} %param.7) | copy-start | bytes 1572868
  10.4 87.0 %collective-permute-start = (f32[3,4,1,512]{3,1,2,0:T(4,128)}, f32[3,4,1,512]{3,1,2,0:T(4,128)S(1)}, u32[]{:S(2)}, u32[]{:S(2)}) collective-permute-start(f32[3,4,1,512]{3,1,2,0:T(4,128)} %copy.1167), channel_id=1, source_target_pairs={{0,8},{8,16},{16,24},{24,32},{32,40},{40,48},{48,56},{56,64},{64,7... | collective-permute-start | bytes 73736 | tf_op jit(solution)/shard_map/ppermute | solution.py:19
  49.9 15.4 %copy-start.38 = (bf16[2,9,64,3]{2,0,3,1:T(2,128)(2,1)S(1)}, bf16[2,9,64,3]{2,0,3,1:T(2,128)(2,1)}, u32[]{:S(2)}) copy-start(bf16[2,9,64,3]{2,0,3,1:T(2,128)(2,1)} %param.11) | copy-start | bytes 20740
  60.6 11.2 %all-to-all-start = ((bf16[3,4,8,128]{3,2,0,1:T(8,128)(2,1)}), bf16[3,4,8,128]{3,2,0,1:T(8,128)(2,1)S(1)}, u32[]{:S(2)}, u32[]{:S(2)}) async-start(bf16[3,4,8,128]{3,2,0,1:T(8,128)(2,1)} %copy.828), calls=%async_computation | async-start | bytes 49152 | tf_op jit(solution)/shard_map/all_to_all | solution.py:80
  70.4 63.5 %copy-start.10 = (f32[1,4,32,512]{2,3,1,0:T(8,128)}, f32[1,4,32,512]{2,3,1,0:T(8,128)S(1)}, u32[]{:S(2)}) copy-start(f32[1,4,32,512]{2,3,1,0:T(8,128)S(1)} %copy.1049) | copy-start | bytes 786436
  71.8 6.6 all-to-all-start.2
  75.1 5.2 collective-permute-start.4
  79.0 4.3 collective-permute-start.5
  90.6 50.1 %collective-permute-start.6 = (bf16[2,64,1,1,512]{4,1,0,3,2:T(8,128)(2,1)}, bf16[2,64,1,1,512]{4,1,0,3,2:T(8,128)(2,1)}, u32[]{:S(2)}, u32[]{:S(2)}) collective-permute-start(bf16[2,64,1,1,512]{4,1,0,3,2:T(8,128)(2,1)} %get-tuple-element.62), channel_id=1, source_target_pairs={{0,8},{8,16},{16,24},{24,32},{32,40},{40,48},{48,56},{56,64},{64,7... | collective-permute-start | bytes 393224 | tf_op jit(solution)/shard_map/ppermute | solution.py:19
  96.1 44.6 %collective-permute-start.7 = (bf16[2,64,1,1,512]{4,1,0,3,2:T(8,128)(2,1)}, bf16[2,64,1,1,512]{4,1,0,3,2:T(8,128)(2,1)}, u32[]{:S(2)}, u32[]{:S(2)}) collective-permute-start(bf16[2,64,1,1,512]{4,1,0,3,2:T(8,128)(2,1)} %get-tuple-element.63), channel_id=1, source_target_pairs={{8,0},{16,8},{24,16},{32,24},{40,32},{48,40},{56,48},{64,56},{72,6... | collective-permute-start | bytes 393224 | tf_op jit(solution)/shard_map/ppermute | solution.py:20
  98.8 10.1 %collective-permute-start.2 = (f32[3,4,34,1]{3,1,2,0:T(4,128)}, f32[3,4,34,1]{3,1,2,0:T(4,128)S(1)}, u32[]{:S(2)}, u32[]{:S(2)}) collective-permute-start(f32[3,4,34,1]{3,1,2,0:T(4,128)} %get-tuple-element.68), channel_id=1, source_target_pairs={{0,2},{2,4},{4,6},{6,0},{1,3},{3,5},{5,7},{7,1},{8,10},{10,12},{12... | collective-permute-start | bytes 4904 | tf_op jit(solution)/shard_map/ppermute | solution.py:19
  101.9 7.1 collective-permute-start.3
  124.9 11.2 %copy-start.23 = (f32[1,4,32,512]{2,3,1,0:T(8,128)S(1)}, f32[1,4,32,512]{2,3,1,0:T(8,128)}, u32[]{:S(2)}) copy-start(f32[1,4,32,512]{2,3,1,0:T(8,128)} %copy.1081) | copy-start | bytes 786436
  149.7 32.1 %copy-start.3 = (bf16[2,8,512,64]{2,3,0,1:T(8,128)(2,1)}, bf16[2,8,512,64]{2,3,0,1:T(8,128)(2,1)S(1)}, u32[]{:S(2)}) copy-start(bf16[2,8,512,64]{2,3,0,1:T(8,128)(2,1)S(1)} %tanh_convert_fusion) | copy-start | bytes 3145732
  150.5 9.5 %collective-permute-start.9 = (bf16[2,64,1,1,512]{4,1,0,3,2:T(8,128)(2,1)}, bf16[2,64,1,1,512]{4,1,0,3,2:T(8,128)(2,1)}, u32[]{:S(2)}, u32[]{:S(2)}) collective-permute-start(bf16[2,64,1,1,512]{4,1,0,3,2:T(8,128)(2,1)} %get-tuple-element.60), channel_id=1, source_target_pairs={{8,0},{16,8},{24,16},{32,24},{40,32},{48,40},{56,48},{64,56},{72,6... | collective-permute-start | bytes 393224 | tf_op jit(solution)/shard_map/ppermute | solution.py:20
  151.7 8.2 %collective-permute-start.8 = (bf16[2,64,1,1,512]{4,1,0,3,2:T(8,128)(2,1)}, bf16[2,64,1,1,512]{4,1,0,3,2:T(8,128)(2,1)}, u32[]{:S(2)}, u32[]{:S(2)}) collective-permute-start(bf16[2,64,1,1,512]{4,1,0,3,2:T(8,128)(2,1)} %get-tuple-element.61), channel_id=1, source_target_pairs={{0,8},{8,16},{16,24},{24,32},{32,40},{40,48},{48,56},{56,64},{64,7... | collective-permute-start | bytes 393224 | tf_op jit(solution)/shard_map/ppermute | solution.py:19
  189.1 13.3 %collective-permute-start.10 = (bf16[2,2,1,1,512]{4,1,3,0,2:T(2,128)(2,1)S(1)}, bf16[2,2,1,1,512]{4,1,3,0,2:T(2,128)(2,1)S(1)}, u32[]{:S(2)}, u32[]{:S(2)}) collective-permute-start(bf16[2,2,1,1,512]{4,1,3,0,2:T(2,128)(2,1)S(1)} %get-tuple-element.90), channel_id=1, source_target_pairs={{0,8},{8,16},{16,24},{24,32},{32,40},{40,48},{48,56},{56,64},{64,7... | collective-permute-start | bytes 12296 | tf_op jit(solution)/shard_map/ppermute | solution.py:19
  193.1 9.3 %collective-permute-start.11 = (bf16[2,2,1,1,512]{4,1,3,0,2:T(2,128)(2,1)S(1)}, bf16[2,2,1,1,512]{4,1,3,0,2:T(2,128)(2,1)S(1)}, u32[]{:S(2)}, u32[]{:S(2)}) collective-permute-start(bf16[2,2,1,1,512]{4,1,3,0,2:T(2,128)(2,1)S(1)} %get-tuple-element.91), channel_id=1, source_target_pairs={{8,0},{16,8},{24,16},{32,24},{40,32},{48,40},{56,48},{64,56},{72,6... | collective-permute-start | bytes 12296 | tf_op jit(solution)/shard_map/ppermute | solution.py:20
  195.4 36.5 %all-to-all-start.1 = ((bf16[4,2,1024]{2,1,0:T(2,128)(2,1)}), bf16[4,2,1024]{2,1,0:T(2,128)(2,1)S(1)}, u32[]{:S(2)}, u32[]{:S(2)}) async-start(bf16[4,2,1024]{2,1,0:T(2,128)(2,1)} %reshape.521), calls=%async_computation.1 | async-start | bytes 32768 | tf_op jit(solution)/shard_map/all_to_all | solution.py:103
  202.0 545.5 %all-reduce.3.cloned.1.call-start = ((), (), s32[]{:S(2)}) async-start(), calls=%async_computation.3 | async-start | bytes 1179648 | tf_op jit(solution)/shard_map/psum | solution.py:129
  214.0 38.2 %collective-permute-start.13 = (bf16[2,64,1,1,512]{4,1,0,3,2:T(8,128)(2,1)}, bf16[2,64,1,1,512]{4,1,0,3,2:T(8,128)(2,1)}, u32[]{:S(2)}, u32[]{:S(2)}) collective-permute-start(bf16[2,64,1,1,512]{4,1,0,3,2:T(8,128)(2,1)} %get-tuple-element.56), channel_id=1, source_target_pairs={{8,0},{16,8},{24,16},{32,24},{40,32},{48,40},{56,48},{64,56},{72,6... | collective-permute-start | bytes 393224 | tf_op jit(solution)/shard_map/ppermute | solution.py:20
  215.3 36.9 %collective-permute-start.12 = (bf16[2,64,1,1,512]{4,1,0,3,2:T(8,128)(2,1)}, bf16[2,64,1,1,512]{4,1,0,3,2:T(8,128)(2,1)}, u32[]{:S(2)}, u32[]{:S(2)}) collective-permute-start(bf16[2,64,1,1,512]{4,1,0,3,2:T(8,128)(2,1)} %get-tuple-element.57), channel_id=1, source_target_pairs={{0,8},{8,16},{16,24},{24,32},{32,40},{40,48},{48,56},{56,64},{64,7... | collective-permute-start | bytes 393224 | tf_op jit(solution)/shard_map/ppermute | solution.py:19
  (36 other events, 177.3 us)
Sparse Core Ops, SparseCore 0:
  232.0 515.4 all-reduce.2
where the time goes:
time: 768 us; the launch traced here: 756 us
  blocking collectives  285 us (37%)
  waiting for transfers between devices  206 us (27%)
  local copies, waits for them, and re-layouts  99.1 us (13%)
  matrix products  61.4 us (8%)
  starting transfers between devices  55 us (7%)
  other arithmetic  34.7 us (5%)
  between operations  15.3 us (2%)
    psum x1, blocking collectives, per_device(): lax.psum((grad_one, grad_two, grad_three), ('lat', 'lon'))  275 us
    psum x1, waiting for transfers between devices, per_device(): lax.psum((grad_one, grad_two, grad_three), ('lat', 'lon'))  203 us
    concatenate x5, local copies, waits for them, and re-layouts, per_device(): fields = jnp.concatenate([velo, temp[None]], 0)  46.9 us
    dot_general x45, matrix products, conv_sum(): jnp.einsum(form, weights[:, k], piece, preferred_element_type=jnp.float32)  36 us
    ppermute x7, starting transfers between devices, with_halo(): before = lax.ppermute(last, axis, up)  32.3 us
    unnamed x107, local copies, waits for them, and re-layouts  28.4 us
    dot_general x27, matrix products, weight_grad(): jnp.einsum(form, cotangent, piece, preferred_element_type=jnp.float32)  25.5 us
  transfers between devices with their start and end apart: 18, of which 2 were waited for; matrix products, arithmetic and copies ran while one was open for 21% of the time, Pallas kernels for 0%

commit v1 on v0

v1 whole, which is shorter than its diff:
```python
import functools
import math

import jax
import jax.numpy as jnp
from jax import lax
from jax.experimental import pallas as pl
from jax.experimental.pallas import tpu as pltpu
from jax.sharding import PartitionSpec as P

LEV = 4
COARSE = 4
HID = 64
HALO = 5
MESH = pl.DeviceIdType.MESH
F32 = jnp.float32
BF16 = jnp.bfloat16
MID_ROWS = 9 * HID
SMALL_ROWS = 72
GRAD_ROWS = MID_ROWS + 2 * SMALL_ROWS
NT = (((1,), (1,)), ((), ()))


def chunking(group):
    tiles = GRAD_ROWS // 8
    per = -(-tiles // group)
    owners = -(-tiles // per)
    return per * 8, owners


def shift_cols(value, by):
    return pltpu.roll(value, by % value.shape[-1], axis=value.ndim - 1)


def kernel(
    n_lat, n_lon, n_mem,
    velo, temp, land, target, w1, w2, w2t, wl, w3t,
    velo_out, temp_out, grads,
    narrow, tall, staged, send_buf, rx, s0, s1, h2s, g3s, d2s, pred_buf, force_rx, force_up, pad,
    row_send, row_rx, col_send, col_rx, acc_mid, acc_first, acc_last, partial, scattered,
    cs_sem, cr_sem, os_sem, or_sem, fs_sem, fr_sem, fl_sem, rs_send, rs_recv, ag_send, ag_recv,
):
    lat = lax.axis_index("lat")
    lon = lax.axis_index("lon")
    mem = lax.axis_index("mem")
    rows = temp.shape[1]
    cols = temp.shape[2]
    rc = rows // COARSE
    cc = cols // COARSE
    width = cc * n_lon
    nyc = rc * n_lat
    group = n_lat * n_lon
    chunk, owners = chunking(group)
    me = lat * n_lon + lon

    def at(lat_to, lon_to, mem_to):
        return {"lat": lat_to, "lon": lon_to, "mem": mem_to}

    def of_group(index):
        return at(index // n_lon, lax.rem(index, n_lon), mem)

    barrier = pltpu.get_barrier_semaphore()

    def greet(i, carry):
        pl.semaphore_signal(
            barrier, inc=1, device_id=of_group(lax.rem(me + i, group)), device_id_type=MESH
        )
        return carry

    lax.fori_loop(1, group, greet, 0)
    for other in range(1, n_mem):
        for l in range(n_lon):
            pl.semaphore_signal(
                barrier, inc=1, device_id=at(lat, l, lax.rem(mem + other, n_mem)), device_id_type=MESH
            )

    q_ids = lax.broadcasted_iota(jnp.int32, (cc, cols), 0)
    i_ids = lax.broadcasted_iota(jnp.int32, (cc, cols), 1)
    expand = jnp.where(i_ids // COARSE == q_ids, 1.0, 0.0).astype(F32)

    def field(c, l, where):
        return velo[c, l, where, :] if c < 2 else temp[l, where, :]

    staged[...] = jnp.zeros_like(staged)
    for c in range(3):
        fine = (velo[c] if c < 2 else temp[...]).reshape(LEV * rows, cols)
        narrow[...] = lax.dot_general(
            fine * (1.0 / COARSE**2), expand, NT,
            precision=lax.Precision.HIGHEST, preferred_element_type=F32,
        )
        pooled = narrow[pl.ds(0, LEV * rc, stride=COARSE), :]
        for r in range(1, COARSE):
            pooled = pooled + narrow[pl.ds(r, LEV * rc, stride=COARSE), :]
        staged[pl.ds(c, LEV * rc, stride=8), :] = pooled
    for c in range(2):
        goal = target[c].astype(F32).reshape(LEV * rc, cc)
        staged[pl.ds(4 + c, LEV * rc, stride=8), :] = goal
        staged[pl.ds(6 + c, LEV * rc, stride=8), :] = goal
    send_buf[...] = staged[...].astype(BF16).reshape(send_buf.shape)

    lane = lax.broadcasted_iota(jnp.int32, (rows, 128), 1)
    west_cols = jnp.zeros((rows, 128), F32)
    east_cols = jnp.zeros((rows, 128), F32)
    for c in range(3):
        for l in range(LEV):
            q = c * LEV + l
            first = velo[c, l, :, 0:128] if c < 2 else temp[l, :, 0:128]
            last = velo[c, l, :, cols - 128 : cols] if c < 2 else temp[l, :, cols - 128 : cols]
            west_cols = jnp.where(lane == q, jnp.broadcast_to(first[:, 0:1], (rows, 128)), west_cols)
            east_cols = jnp.where(lane == q, jnp.broadcast_to(last[:, 127:128], (rows, 128)), east_cols)
            row_send[0, q : q + 1, :] = field(c, l, pl.ds(0, 1))
            row_send[1, q : q + 1, :] = field(c, l, pl.ds(rows - 1, 1))
            pad[q, 8 : 8 + rows, :] = field(c, l, pl.ds(0, rows))
    col_send[0] = west_cols
    col_send[1] = east_cols

    @pl.when(lat == 0)
    def _():
        rx[:, 0:HALO] = jnp.zeros((n_lon, HALO, 8, cc), BF16)
        row_rx[0] = jnp.zeros_like(row_rx[0])

    @pl.when(lat == n_lat - 1)
    def _():
        rx[:, HALO + rc : 2 * HALO + rc] = jnp.zeros((n_lon, HALO, 8, cc), BF16)
        row_rx[1] = jnp.zeros_like(row_rx[1])

    pl.semaphore_wait(barrier, group - 1 + (n_mem - 1) * n_lon)

    def own_copy(l):
        return pltpu.make_async_remote_copy(
            src_ref=send_buf.at[l], dst_ref=rx.at[lon, pl.ds(HALO, rc)],
            send_sem=cs_sem.at[0, l], recv_sem=cr_sem.at[0, lon],
            device_id=at(lat, l, mem), device_id_type=MESH,
        )

    def up_copy(l):
        return pltpu.make_async_remote_copy(
            src_ref=send_buf.at[l, pl.ds(rc - HALO, HALO)], dst_ref=rx.at[lon, pl.ds(0, HALO)],
            send_sem=cs_sem.at[1, l], recv_sem=cr_sem.at[1, lon],
            device_id=at(lat + 1, l, mem), device_id_type=MESH,
        )

    def down_copy(l):
        return pltpu.make_async_remote_copy(
            src_ref=send_buf.at[l, pl.ds(0, HALO)], dst_ref=rx.at[lon, pl.ds(HALO + rc, HALO)],
            send_sem=cs_sem.at[2, l], recv_sem=cr_sem.at[2, lon],
            device_id=at(lat - 1, l, mem), device_id_type=MESH,
        )

    def row_up():
        return pltpu.make_async_remote_copy(
            src_ref=row_send.at[1], dst_ref=row_rx.at[0], send_sem=os_sem.at[0], recv_sem=or_sem.at[0],
            device_id=at(lat + 1, lon, mem), device_id_type=MESH,
        )

    def row_down():
        return pltpu.make_async_remote_copy(
            src_ref=row_send.at[0], dst_ref=row_rx.at[1], send_sem=os_sem.at[1], recv_sem=or_sem.at[1],
            device_id=at(lat - 1, lon, mem), device_id_type=MESH,
        )

    def col_east():
        return pltpu.make_async_remote_copy(
            src_ref=col_send.at[1], dst_ref=col_rx.at[0], send_sem=os_sem.at[2], recv_sem=or_sem.at[2],
            device_id=at(lat, lax.rem(lon + 1, n_lon), mem), device_id_type=MESH,
        )

    def col_west():
        return pltpu.make_async_remote_copy(
            src_ref=col_send.at[0], dst_ref=col_rx.at[1], send_sem=os_sem.at[3], recv_sem=or_sem.at[3],
            device_id=at(lat, lax.rem(lon + n_lon - 1, n_lon), mem), device_id_type=MESH,
        )

    for l in range(n_lon):
        @pl.when(lat < n_lat - 1)
        def _(l=l):
            up_copy(l).start()

        @pl.when(lat > 0)
        def _(l=l):
            down_copy(l).start()

        @pl.when(lon != l)
        def _(l=l):
            own_copy(l).start()

    @pl.when(lat < n_lat - 1)
    def _():
        row_up().start()

    @pl.when(lat > 0)
    def _():
        row_down().start()

    col_east().start()
    col_west().start()

    rx[lon, HALO : HALO + rc] = send_buf[lon]
    acc_mid[...] = jnp.zeros_like(acc_mid)
    acc_first[...] = jnp.zeros_like(acc_first)
    acc_last[...] = jnp.zeros_like(acc_last)

    def arrived(kind, l, src, dst):
        pltpu.make_async_copy(src, dst, cr_sem.at[kind, l]).wait()

    for l in range(n_lon):
        @pl.when(lon != l)
        def _(l=l):
            arrived(0, l, send_buf.at[l], rx.at[l, pl.ds(HALO, rc)])

        @pl.when(lat > 0)
        def _(l=l):
            arrived(1, l, send_buf.at[l, pl.ds(0, HALO)], rx.at[l, pl.ds(0, HALO)])

        @pl.when(lat < n_lat - 1)
        def _(l=l):
            arrived(2, l, send_buf.at[l, pl.ds(0, HALO)], rx.at[l, pl.ds(HALO + rc, HALO)])

    def inside(g):
        return jnp.where(jnp.logical_and(g >= 0, g < nyc), 1.0, 0.0).astype(F32)

    def received(x):
        return jnp.concatenate([rx[l, x].astype(F32) for l in range(n_lon)], axis=-1)

    def fill_s0(x, carry):
        v = received(x)
        s0[x] = jnp.concatenate(
            [shift_cols(v, 1), v, shift_cols(v, -1), jnp.zeros_like(v)], axis=0
        ).astype(BF16)
        return carry

    lax.fori_loop(0, rc + 2 * HALO, fill_s0, 0)

    def first_layer(r, carry):
        block = s0[pl.ds(r, 3)].reshape(96, width)
        h = jnp.tanh(jnp.dot(w1[...], block, preferred_element_type=F32)) * inside(lat * rc - 4 + r)
        for m in range(2):
            hm = h[m * HID : (m + 1) * HID]
            s1[m, r, 0:HID] = shift_cols(hm, 1).astype(BF16)
            s1[m, r, HID : 2 * HID] = hm.astype(BF16)
            s1[m, r, 2 * HID : 3 * HID] = shift_cols(hm, -1).astype(BF16)
        return carry

    lax.fori_loop(0, rc + 8, first_layer, 0)

    def second_layer(r, carry):
        keep = inside(lat * rc - 3 + r)
        for m in range(2):
            block = s1[m, pl.ds(r, 3)].reshape(9 * HID, width)
            h = jnp.tanh(jnp.dot(w2[m], block, preferred_element_type=F32)) * keep
            h2s[r, m * HID : (m + 1) * HID] = h.astype(BF16)
        return carry

    lax.fori_loop(0, rc + 6, second_layer, 0)

    scale = 2.0 / (2.0 * LEV * nyc * width)
    sub = lax.broadcasted_iota(jnp.int32, (8, width), 0)

    def last_layer(r, carry):
        block = h2s[pl.ds(r, 3)].reshape(6 * HID, width)
        u = jnp.dot(wl[...], block, preferred_element_type=F32)
        pred = shift_cols(u[0:8], 1) + u[8:16] + shift_cols(u[16:24], -1)
        g3 = jnp.where(sub >= 4, (pred - received(r + 3)) * scale, 0.0) * inside(lat * rc - 2 + r)
        g3s[r] = jnp.concatenate(
            [shift_cols(g3, -1), g3, shift_cols(g3, 1), jnp.zeros_like(g3)], axis=0
        ).astype(BF16)
        both = pred[4:6] + pred[6:8]

        @pl.when(jnp.logical_and(r >= 2, r < 2 + rc))
        def _():
            for o in range(2):
                pred_buf[o, pl.ds(r - 2, 1), :] = both[o : o + 1]

        return carry

    lax.fori_loop(0, rc + 4, last_layer, 0)

    def force_copy(l, m):
        return pltpu.make_async_remote_copy(
            src_ref=pred_buf.at[:, :, pl.ds(l * cc, cc)], dst_ref=force_rx.at[mem, lon],
            send_sem=fs_sem.at[m, l], recv_sem=fr_sem.at[mem, lon],
            device_id=at(lat, l, m), device_id_type=MESH,
        )

    def force_own():
        return pltpu.make_async_copy(
            pred_buf.at[:, :, pl.ds(pl.multiple_of(lon * cc, cc), cc)], force_rx.at[mem, lon], fl_sem
        )

    def elsewhere(l, m):
        return jnp.logical_or(lon != l, mem != m)

    for m in range(n_mem):
        for l in range(n_lon):
            @pl.when(elsewhere(l, m))
            def _(l=l, m=m):
                force_copy(l, m).start()

    force_own().start()

    def back_second(r, carry):
        block = g3s[pl.ds(r, 3)].reshape(96, width)
        h = h2s[r + 2].astype(F32)
        d = jnp.dot(w3t[...], block, preferred_element_type=F32) * (1.0 - h * h)
        d = d * inside(lat * rc - 1 + r)
        for m in range(2):
            dm = d[m * HID : (m + 1) * HID]
            d2s[m, r, 0:HID] = shift_cols(dm, -1).astype(BF16)
            d2s[m, r, HID : 2 * HID] = dm.astype(BF16)
            d2s[m, r, 2 * HID : 3 * HID] = shift_cols(dm, 1).astype(BF16)
        return carry

    lax.fori_loop(0, rc + 2, back_second, 0)

    def own_row(r, carry):
        ups = g3s[pl.ds(r + 1, 3)].reshape(96, width)
        acc_last[...] += lax.dot_general(ups, h2s[r + 3], NT, preferred_element_type=F32)
        parts = []
        for m in range(2):
            hidden = s1[m, pl.ds(r + 3, 3), HID : 2 * HID]
            acc_mid[m] += lax.dot_general(
                d2s[m, r + 1], hidden.reshape(3 * HID, width), NT, preferred_element_type=F32
            )
            block = d2s[m, pl.ds(r, 3)].reshape(9 * HID, width)
            h = s1[m, r + 4, HID : 2 * HID].astype(F32)
            d = jnp.dot(w2t[m], block, preferred_element_type=F32) * (1.0 - h * h)
            parts.append(d.astype(BF16))
        d1 = jnp.concatenate(parts, axis=0)
        xs = s0[pl.ds(r + 4, 3)].reshape(96, width)
        acc_first[...] += lax.dot_general(xs, d1, NT, preferred_element_type=F32)
        return carry

    lax.fori_loop(0, rc, own_row, 0)

    for a in range(3):
        partial[a * 192 : (a + 1) * 192, :] = jnp.concatenate(
            [acc_mid[m, :, a * HID : (a + 1) * HID] for m in range(2)], axis=-1
        )
        partial[MID_ROWS + 24 * a : MID_ROWS + 24 * a + 24, :] = acc_first[32 * a : 32 * a + 24, :]
        at_row = MID_ROWS + SMALL_ROWS + 24 * a
        partial[at_row : at_row + 24, :] = acc_last[32 * a : 32 * a + 24, :]
    if owners * chunk > GRAD_ROWS:
        partial[GRAD_ROWS:, :] = jnp.zeros((owners * chunk - GRAD_ROWS, 128), F32)

    def piece(ref, index):
        return ref.at[pl.ds(pl.multiple_of(index * chunk, chunk), chunk)]

    def scatter(i, carry):
        to = lax.rem(me + i, group)

        @pl.when(to < owners)
        def _():
            pltpu.make_async_remote_copy(
                src_ref=piece(partial, to), dst_ref=scattered.at[i - 1],
                send_sem=rs_send, recv_sem=rs_recv, device_id=of_group(to), device_id_type=MESH,
            ).start()

        return carry

    lax.fori_loop(1, group, scatter, 0)

    for m in range(n_mem):
        for l in range(n_lon):
            @pl.when(elsewhere(l, m))
            def _(l=l, m=m):
                pltpu.make_async_copy(
                    pred_buf.at[:, :, pl.ds(0, cc)], force_rx.at[m, l], fr_sem.at[m, l]
                ).wait()

    force_own().wait()

    @pl.when(lat > 0)
    def _():
        pltpu.make_async_copy(row_send.at[0], row_rx.at[0], or_sem.at[0]).wait()

    @pl.when(lat < n_lat - 1)
    def _():
        pltpu.make_async_copy(row_send.at[0], row_rx.at[1], or_sem.at[1]).wait()

    pltpu.make_async_copy(col_send.at[0], col_rx.at[0], or_sem.at[2]).wait()
    pltpu.make_async_copy(col_send.at[0], col_rx.at[1], or_sem.at[3]).wait()

    summed = force_rx[0]
    for m in range(1, n_mem):
        summed = summed + force_rx[m]
    mean = (summed * (1.0 / (2 * n_mem))).reshape(LEV * 2 * rc, cc)
    for r in range(COARSE):
        tall[pl.ds(r, LEV * 2 * rc, stride=COARSE), :] = mean
    force_up[...] = jnp.dot(
        tall[...], expand, precision=lax.Precision.HIGHEST, preferred_element_type=F32
    ).reshape(force_up.shape)
    for q in range(3 * LEV):
        pad[q, 7:8, :] = row_rx[0, q : q + 1, :]
        pad[q, 8 + rows : 9 + rows, :] = row_rx[1, q : q + 1, :]

    lane_ids = lax.broadcasted_iota(jnp.int32, (8, cols), 1)
    for s in range(rows // 8):
        base = 8 + 8 * s
        ids = (lat * rows + 8 * s + lax.broadcasted_iota(jnp.int32, (8, cols), 0)).astype(F32)
        coriolis = jnp.sin(-math.pi / 2 + math.pi * (ids + 0.5) / (rows * n_lat))
        wet = 0.1 * land[8 * s : 8 * s + 8, :].astype(F32)
        sum_x = jnp.zeros((8, cols), F32)
        sum_y = jnp.zeros((8, cols), F32)
        for l in range(LEV):
            got = []
            for c in range(3):
                q = c * LEV + l
                centre = pad[q, base : base + 8, :]
                south = pad[q, base - 1 : base + 7, :]
                north = pad[q, base + 1 : base + 9, :]
                before = col_rx[0, 8 * s : 8 * s + 8, q : q + 1]
                after = col_rx[1, 8 * s : 8 * s + 8, q : q + 1]
                west = jnp.where(lane_ids == 0, before, shift_cols(centre, 1))
                east = jnp.where(lane_ids == cols - 1, after, shift_cols(centre, -1))
                got.append((centre, east, west, north, south))
            laps = [e + w + n + so - 4.0 * ce for ce, e, w, n, so in got]
            u, v, t = got[0][0], got[1][0], got[2][0]
            dx = got[2][1] - got[2][2]
            dy = got[2][3] - got[2][4]
            sum_x = sum_x + dx
            sum_y = sum_y + dy
            fu = force_up[l * 2, 8 * s : 8 * s + 8, :]
            fv = force_up[l * 2 + 1, 8 * s : 8 * s + 8, :]
            velo_out[0, l, 8 * s : 8 * s + 8, :] = u + wet * (
                coriolis * v + 0.25 * sum_x + 0.5 * laps[0] + fu
            )
            velo_out[1, l, 8 * s : 8 * s + 8, :] = v + wet * (
                -coriolis * u + 0.25 * sum_y + 0.5 * laps[1] + fv
            )
            temp_out[l, 8 * s : 8 * s + 8, :] = t + wet * (
                -0.5 * (u * dx + v * dy) + 0.3 * laps[2]
            )

    def passed(ref, count, sem):
        pltpu.make_async_copy(ref.at[pl.ds(0, count)], ref.at[pl.ds(0, count)], sem).wait()

    @pl.when(me < owners)
    def _():
        passed(scattered, group - 1, rs_recv)

        def add(i, total):
            return total + scattered[i]

        start = pl.multiple_of(me * chunk, chunk)
        grads[pl.ds(start, chunk), :] = lax.fori_loop(
            0, group - 1, add, partial[pl.ds(start, chunk), :]
        )

        def gather(i, carry):
            pltpu.make_async_remote_copy(
                src_ref=piece(grads, me), dst_ref=piece(grads, me),
                send_sem=ag_send, recv_sem=ag_recv,
                device_id=of_group(lax.rem(me + i, group)), device_id_type=MESH,
            ).start()
            return carry

        lax.fori_loop(1, group, gather, 0)

    for l in range(n_lon):
        @pl.when(lat < n_lat - 1)
        def _(l=l):
            up_copy(l).wait_send()

        @pl.when(lat > 0)
        def _(l=l):
            down_copy(l).wait_send()

        @pl.when(lon != l)
        def _(l=l):
            own_copy(l).wait_send()

        for m in range(n_mem):
            @pl.when(elsewhere(l, m))
            def _(l=l, m=m):
                force_copy(l, m).wait_send()

    @pl.when(lat < n_lat - 1)
    def _():
        row_up().wait_send()

    @pl.when(lat > 0)
    def _():
        row_down().wait_send()

    col_east().wait_send()
    col_west().wait_send()

    @pl.when(me < owners)
    def _():
        passed(partial, (owners - 1) * chunk, rs_send)
        passed(grads, (owners - 1) * chunk, ag_recv)
        passed(scattered, group - 1, ag_send)

    @pl.when(me >= owners)
    def _():
        passed(partial, owners * chunk, rs_send)
        passed(grads, owners * chunk, ag_recv)


def per_device(n_lat, n_lon, n_mem, velo, temp, land, target, w_first, w_middle, w_last):
    rows, cols = temp.shape[1], temp.shape[2]
    rc, cc = rows // COARSE, cols // COARSE
    width = cc * n_lon
    group = n_lat * n_lon
    chunk, owners = chunking(group)
    mine = w_first.shape[0]

    wf = w_first.reshape(mine, 3, 3, HID, 3)
    wm = w_middle.reshape(mine, 3, 3, HID, HID)
    wo = w_last.reshape(mine, 3, 3, 2, HID)
    w1 = jnp.pad(jnp.transpose(wf, (0, 3, 1, 2, 4)), ((0, 0), (0, 0), (0, 0), (0, 1), (0, 5)))
    w1 = w1.reshape(mine * HID, 96)
    w2 = jnp.transpose(wm, (0, 3, 1, 2, 4)).reshape(mine, HID, 9 * HID)
    w2t = jnp.transpose(wm[:, ::-1], (0, 4, 1, 2, 3)).reshape(mine, HID, 9 * HID)
    eye = jnp.eye(mine, dtype=BF16)
    wl = jnp.pad(
        jnp.einsum("mabox,mn->bnoamx", wo, eye).reshape(3, 4, 6 * HID), ((0, 0), (4, 0), (0, 0))
    ).reshape(24, 6 * HID)
    w3t = jnp.pad(
        jnp.einsum("mabox,mn->mxabno", wo[:, ::-1], eye).reshape(mine * HID, 3, 3, 4),
        ((0, 0), (0, 0), (0, 1), (4, 0)),
    ).reshape(mine * HID, 96)

    vmem = pl.BlockSpec(memory_space=pltpu.VMEM)
    dma = pltpu.SemaphoreType.DMA
    velo_next, temp_next, grads = pl.pallas_call(
        functools.partial(kernel, n_lat, n_lon, n_mem),
        out_shape=(
            jax.ShapeDtypeStruct(velo.shape, F32),
            jax.ShapeDtypeStruct(temp.shape, F32),
            jax.ShapeDtypeStruct((owners * chunk, 128), F32),
        ),
        in_specs=[vmem] * 9,
        out_specs=(vmem, vmem, vmem),
        scratch_shapes=[
            pltpu.VMEM((LEV * rows, cc), F32),
            pltpu.VMEM((LEV * 2 * rows, cc), F32),
            pltpu.VMEM((LEV * rc * 8, cc), F32),
            pltpu.VMEM((LEV, rc, 8, cc), BF16),
            pltpu.VMEM((n_lon, rc + 2 * HALO, 8, cc), BF16),
            pltpu.VMEM((rc + 2 * HALO, 32, width), BF16),
            pltpu.VMEM((2, rc + 8, 3 * HID, width), BF16),
            pltpu.VMEM((rc + 6, 2 * HID, width), BF16),
            pltpu.VMEM((rc + 4, 32, width), BF16),
            pltpu.VMEM((2, rc + 2, 3 * HID, width), BF16),
            pltpu.VMEM((2, rc, width), F32),
            pltpu.VMEM((n_mem, n_lon, 2, rc, cc), F32),
            pltpu.VMEM((LEV * 2, rows, cols), F32),
            pltpu.VMEM((3 * LEV, rows + 16, cols), F32),
            pltpu.VMEM((2, 16, cols), F32),
            pltpu.VMEM((2, 16, cols), F32),
            pltpu.VMEM((2, rows, 128), F32),
            pltpu.VMEM((2, rows, 128), F32),
            pltpu.VMEM((2, 3 * HID, 3 * HID), F32),
            pltpu.VMEM((96, 128), F32),
            pltpu.VMEM((96, 128), F32),
            pltpu.VMEM((owners * chunk, 128), F32),
            pltpu.VMEM((group - 1, chunk, 128), F32),
            dma((3, n_lon)),
            dma((3, n_lon)),
            dma((4,)),
            dma((4,)),
            dma((n_mem, n_lon)),
            dma((n_mem, n_lon)),
            dma,
            dma,
            dma,
            dma,
            dma,
        ],
        compiler_params=pltpu.CompilerParams(
            collective_id=0, has_side_effects=True, vmem_limit_bytes=56 * 1024 * 1024
        ),
        name="ocean_step",
    )(velo, temp, land, target, w1, w2, w2t, wl, w3t)

    mid = grads[:MID_ROWS].reshape(3, 3, HID, mine, HID)
    grad_middle = jnp.transpose(mid, (3, 0, 1, 2, 4)).reshape(mine, 9, HID, HID)
    first = grads[MID_ROWS : MID_ROWS + SMALL_ROWS].reshape(9, 8, mine, HID)[:, :3]
    grad_first = jnp.transpose(first, (2, 0, 3, 1))
    last = grads[MID_ROWS + SMALL_ROWS : GRAD_ROWS].reshape(3, 3, 8, mine, HID)[::-1, :, 4:]
    last = last.reshape(9, mine, 2, mine, HID)
    grad_last = jnp.stack([last[:, m, :, m] for m in range(mine)], 0)
    return (velo_next, temp_next, grad_first, grad_middle, grad_last)


def solution(mesh):
    return jax.shard_map(
        functools.partial(per_device, mesh.shape["lat"], mesh.shape["lon"], mesh.shape["mem"]),
        mesh=mesh,
        in_specs=(
            P(None, None, "lat", "lon"),
            P(None, "lat", "lon"),
            P("lat", "lon"),
            P(None, None, "lat", "lon"),
            P("mem", None, None, None),
            P("mem", None, None, None),
            P("mem", None, None, None),
        ),
        out_specs=(
            P(None, None, "lat", "lon"),
            P(None, "lat", "lon"),
            P("mem", None, None, None),
            P("mem", None, None, None),
            P("mem", None, None, None),
        ),
        check_vma=False,
    )
```

time: 768 us -> 70.3 us (0.09); the launches traced: 756 us -> 69.9 us
  blocking collectives: 285 us -> 0 us
  waiting for transfers between devices: 206 us -> 0 us
  local copies, waits for them, and re-layouts: 99.1 us -> 11.8 us
  matrix products: 61.4 us -> 0 us
  Pallas kernels: 0 us -> 56.7 us
  starting transfers between devices: 55 us -> 0 us
  other arithmetic: 34.7 us -> 0.72 us
  between operations: 15.3 us -> 0.75 us
    psum x2 -> x0, blocking collectives: 285 us -> none  [the longest x1 275 us: per_device(): lax.psum((grad_one, grad_two, grad_three), ('lat', 'lon'))]
    psum x1 -> x0, waiting for transfers between devices: 203 us -> none  [per_device(): lax.psum((grad_one, grad_two, grad_three), ('lat', 'lon'))]
    dot_general x72 -> x0, matrix products: 61.4 us -> none  [the longest x45 36 us: conv_sum(): jnp.einsum(form, weights[:, k], piece, preferred_element_type=jnp.float32)]
    pallas_call x0 -> x1, Pallas kernels: none -> 56.7 us  [per_device(): pl.pallas_call(functools.partial(kernel, n_lat, n_lon, n_mem), out_shape=...]
    concatenate x7 -> x0, local copies, waits for them, and re-layouts: 46.9 us -> none  [the longest x5 46.9 us: per_device(): fields = jnp.concatenate([velo, temp[None]], 0)]
    ppermute x14 -> x0, starting transfers between devices: 40.2 us -> none  [the longest x7 32.3 us: with_halo(): before = lax.ppermute(last, axis, up)]
    unnamed x107 -> x10, local copies, waits for them, and re-layouts: 28.4 us -> 2.2 us
    concatenate x8 -> x0, other arithmetic: 15.3 us -> none  [the longest x4 7.85 us: pad_cols(): jnp.concatenate([values[..., -1:], values, values[..., :1]], axis=4)]
  transfers between devices with their start and end apart: 18 -> 0, of which waited for: 2 -> 0; matrix products, arithmetic and copies ran while one was open for 21% -> 0% of each run, Pallas kernels for 0% -> 0%
where the time goes in v1:
time: 70.3 us; the launch traced here: 69.9 us
  Pallas kernels  56.7 us (81%)
  local copies, waits for them, and re-layouts  11.8 us (17%)
  between operations  0.75 us (1%)
  other arithmetic  0.72 us (1%)
    pallas_call x1, Pallas kernels, per_device(): pl.pallas_call(functools.partial(kernel, n_lat, n_lon, n_mem), out_shape=...  56.7 us
    unnamed x10, local copies, waits for them, and re-layouts  2.2 us

profile of v1, /device:TPU:1, one launch (start us, length us, event | category | flops | bytes accessed | tf_op | source)
XLA Modules:
  0.0 69.9 jit_solution(9869905613060729012)
XLA Ops:
  0.7 0.8 %rev.10 = bf16[2,3,3,2,64]{4,3,2,1,0:T(2,128)(2,1)S(1)} reverse(bf16[2,3,3,2,64]{4,3,2,1,0:T(2,128)(2,1)} %bitcast.39), dimensions={1} | reverse | bytes 9216 | tf_op jit(solution)/shard_map/rev | solution.py:520
  1.4 0.7 %copy.29 = bf16[2,3,3,2,64]{4,0,3,2,1:T(2,128)(2,1)S(1)} copy(bf16[2,3,3,2,64]{4,3,2,1,0:T(2,128)(2,1)} %bitcast.40) | data formatting | bytes 9216 | tf_op jit(solution)/shard_map/reshape | solution.py:510
  2.1 0.1 multiply_bitcast_fusion
  2.3 0.7 %copy.35.w3t = bf16[128,96]{1,0:T(8,128)(2,1)} copy(bf16[128,96]{0,1:T(8,128)(2,1)S(1)} %bitcast.37) | data formatting | bytes 49152 | tf_op jit(solution)/shard_map/reshape | solution.py:522
  3.1 0.1 reshape.61
  3.2 0.6 pad_bitcast_fusion.wl
  3.9 0.1 reshape.56
  4.0 0.7 %copy.32.w1 = bf16[128,96]{1,0:T(8,128)(2,1)} copy(bf16[128,96]{0,1:T(8,128)(2,1)S(1)} %reshape.56) | data formatting | bytes 49152 | tf_op jit(solution)/shard_map/reshape | solution.py:512
  4.7 0.8 %copy.34.w2t = bf16[2,64,576]{2,1,0:T(8,128)(2,1)} copy(bf16[2,64,576]{1,2,0:T(8,128)(2,1)S(1)} %bitcast.34) | data formatting | bytes 294912 | tf_op jit(solution)/shard_map/reshape | solution.py:514
  5.6 0.2 copy.28
  5.8 0.8 %copy.33.w2 = bf16[2,64,576]{2,1,0:T(8,128)(2,1)} copy(bf16[2,64,576]{1,2,0:T(8,128)(2,1)S(1)} %bitcast.35) | data formatting | bytes 294912 | tf_op jit(solution)/shard_map/reshape | solution.py:513
  6.6 56.7 %ocean_step.1 = (f32[2,4,32,512]{3,2,1,0:T(8,128)}, f32[4,32,512]{2,1,0:T(8,128)}, f32[720,128]{1,0:T(8,128)}) custom-call(f32[2,4,32,512]{3,2,1,0:T(8,128)} %velo.1, f32[4,32,512]{2,1,0:T(8,128)} %temp.1, s32[32,512]{1,0:T(8,128)} %land.1, bf16[2,4,8,128]{3,2,1,0:T(8,128)(2,1)} %target.1, bf16[128,96]{1,0:T(8,128)(2,1)} %copy.32.w1, ...), custom_call_target="tpu_custom_call" | custom-call | tf_op jit(solution)/shard_map/ocean_step/pallas_call | solution.py:526
  63.3 0.8 %fusion = (f32[72,128]{1,0:T(8,128)S(1)}, f32[72,128]{1,0:T(8,128)S(1)}) fusion(f32[720,128]{1,0:T(8,128)} %get-tuple-element.10), kind=kLoop, calls=%fused_computation.6 | loop fusion | bytes 147456 | tf_op jit(solution)/shard_map/slice | solution.py:581
  64.1 1.0 %slice.23 = f32[576,128]{1,0:T(8,128)S(1)} slice(f32[720,128]{1,0:T(8,128)} %get-tuple-element.10), slice={[0:576], [0:128]} | slice | bytes 589824 | tf_op jit(solution)/shard_map/slice | solution.py:577
  65.1 0.1 reshape.68
  65.2 0.6 pad_maximum_fusion
  65.8 0.1 reshape.65
  65.9 0.6 slice_bitcast_fusion
  66.6 0.4 reshape.66
  66.9 0.9 %copy.36 = f32[2,3,3,64,64]{4,3,2,1,0:T(8,128)} copy(f32[2,3,3,64,64]{4,0,3,2,1:T(2,128)S(1)} %bitcast.31) | data formatting | bytes 589824 | tf_op jit(solution)/shard_map/transpose | solution.py:578
  67.8 0.3 copy-done.1
  68.1 0.8 %copy.41 = f32[2,4,32,512]{3,2,1,0:T(8,128)} copy(f32[2,4,32,512]{3,2,1,0:T(8,128)S(1)} %copy-done.1) | data formatting | bytes 1048576
  68.9 0.3 copy-done.2
  69.2 0.7 %copy.42 = f32[4,32,512]{2,1,0:T(8,128)} copy(f32[4,32,512]{2,1,0:T(8,128)S(1)} %copy-done.2) | data formatting | bytes 524288
  (16 shorter events, 0.3 us)
Async XLA Ops:
  0.6 4.1 %copy-start = (bf16[2,9,64,64]{3,2,1,0:T(8,128)(2,1)S(1)}, bf16[2,9,64,64]{3,2,1,0:T(8,128)(2,1)}, u32[]{:S(2)}) copy-start(bf16[2,9,64,64]{3,2,1,0:T(8,128)(2,1)} %param.12) | copy-start | bytes 442372
  3.2 0.7 %copy-start.3 = (bf16[2,9,64,3]{2,0,3,1:T(2,128)(2,1)S(1)}, bf16[2,9,64,3]{2,0,3,1:T(2,128)(2,1)}, u32[]{:S(2)}) copy-start(bf16[2,9,64,3]{2,0,3,1:T(2,128)(2,1)} %param.11) | copy-start | bytes 20740
  66.9 1.2 %copy-start.1 = (f32[2,4,32,512]{3,2,1,0:T(8,128)S(1)}, f32[2,4,32,512]{3,2,1,0:T(8,128)}, u32[]{:S(2)}) copy-start(f32[2,4,32,512]{3,2,1,0:T(8,128)} %get-tuple-element.22) | copy-start | bytes 1572868
  68.1 1.1 %copy-start.2 = (f32[4,32,512]{2,1,0:T(8,128)S(1)}, f32[4,32,512]{2,1,0:T(8,128)}, u32[]{:S(2)}) copy-start(f32[4,32,512]{2,1,0:T(8,128)} %get-tuple-element.23) | copy-start | bytes 786436

commit v2 on v1

--- a/solution.py
+++ b/solution.py
@@ -34,17 +34,19 @@
 
 def kernel(
     n_lat, n_lon, n_mem,
-    velo, temp, land, target, w1, w2, w2t, wl, w3t,
+    velo_in, temp_in, land_in, target_in, w_first, w_middle, w_last,
     velo_out, temp_out, grads,
+    velo_new, temp_new, land, target,
     narrow, tall, staged, send_buf, rx, s0, s1, h2s, g3s, d2s, pred_buf, force_rx, force_up, pad,
-    row_send, row_rx, col_send, col_rx, acc_mid, acc_first, acc_last, partial, scattered,
+    row_send, row_rx, col_send, col_rx, w1_rows, wl_rows, partial, scattered,
+    in_sem, out_sem,
     cs_sem, cr_sem, os_sem, or_sem, fs_sem, fr_sem, fl_sem, rs_send, rs_recv, ag_send, ag_recv,
 ):
     lat = lax.axis_index("lat")
     lon = lax.axis_index("lon")
     mem = lax.axis_index("mem")
-    rows = temp.shape[1]
-    cols = temp.shape[2]
+    rows = temp_in.shape[1]
+    cols = temp_in.shape[2]
     rc = rows // COARSE
     cc = cols // COARSE
     width = cc * n_lon
@@ -59,6 +61,19 @@
     def of_group(index):
         return at(index // n_lon, lax.rem(index, n_lon), mem)
 
+    inner = pl.ds(8, rows)
+    loads = [
+        pltpu.make_async_copy(velo_in.at[c], pad.at[pl.ds(c * LEV, LEV), inner], in_sem.at[c])
+        for c in range(2)
+    ]
+    loads.append(
+        pltpu.make_async_copy(temp_in, pad.at[pl.ds(2 * LEV, LEV), inner], in_sem.at[2])
+    )
+    loads.append(pltpu.make_async_copy(target_in, target, in_sem.at[3]))
+    loads.append(pltpu.make_async_copy(land_in, land, in_sem.at[4]))
+    for load in loads:
+        load.start()
+
     barrier = pltpu.get_barrier_semaphore()
 
     def greet(i, carry):
@@ -78,12 +93,11 @@
     i_ids = lax.broadcasted_iota(jnp.int32, (cc, cols), 1)
     expand = jnp.where(i_ids // COARSE == q_ids, 1.0, 0.0).astype(F32)
 
-    def field(c, l, where):
-        return velo[c, l, where, :] if c < 2 else temp[l, where, :]
-
+    for load in loads[:4]:
+        load.wait()
     staged[...] = jnp.zeros_like(staged)
     for c in range(3):
-        fine = (velo[c] if c < 2 else temp[...]).reshape(LEV * rows, cols)
+        fine = pad[c * LEV : (c + 1) * LEV, 8 : 8 + rows, :].reshape(LEV * rows, cols)
         narrow[...] = lax.dot_general(
             fine * (1.0 / COARSE**2), expand, NT,
             precision=lax.Precision.HIGHEST, preferred_element_type=F32,
@@ -101,16 +115,13 @@
     lane = lax.broadcasted_iota(jnp.int32, (rows, 128), 1)
     west_cols = jnp.zeros((rows, 128), F32)
     east_cols = jnp.zeros((rows, 128), F32)
-    for c in range(3):
-        for l in range(LEV):
-            q = c * LEV + l
-            first = velo[c, l, :, 0:128] if c < 2 else temp[l, :, 0:128]
-            last = velo[c, l, :, cols - 128 : cols] if c < 2 else temp[l, :, cols - 128 : cols]
-            west_cols = jnp.where(lane == q, jnp.broadcast_to(first[:, 0:1], (rows, 128)), west_cols)
-            east_cols = jnp.where(lane == q, jnp.broadcast_to(last[:, 127:128], (rows, 128)), east_cols)
-            row_send[0, q : q + 1, :] = field(c, l, pl.ds(0, 1))
-            row_send[1, q : q + 1, :] = field(c, l, pl.ds(rows - 1, 1))
-            pad[q, 8 : 8 + rows, :] = field(c, l, pl.ds(0, rows))
+    for q in range(3 * LEV):
+        first = pad[q, 8 : 8 + rows, 0:128]
+        last = pad[q, 8 : 8 + rows, cols - 128 : cols]
+        west_cols = jnp.where(lane == q, jnp.broadcast_to(first[:, 0:1], (rows, 128)), west_cols)
+        east_cols = jnp.where(lane == q, jnp.broadcast_to(last[:, 127:128], (rows, 128)), east_cols)
+        row_send[0, q : q + 1, :] = pad[q, 8:9, :]
+        row_send[1, q : q + 1, :] = pad[q, 7 + rows : 8 + rows, :]
     col_send[0] = west_cols
     col_send[1] = east_cols
 
@@ -196,9 +207,44 @@
     col_west().start()
 
     rx[lon, HALO : HALO + rc] = send_buf[lon]
-    acc_mid[...] = jnp.zeros_like(acc_mid)
-    acc_first[...] = jnp.zeros_like(acc_first)
-    acc_last[...] = jnp.zeros_like(acc_last)
+    def flip(matrix):
+        size = matrix.shape[1]
+        eye = jnp.where(
+            lax.broadcasted_iota(jnp.int32, (size, size), 0)
+            == lax.broadcasted_iota(jnp.int32, (size, size), 1),
+            1.0, 0.0,
+        ).astype(BF16)
+        return lax.dot_general(eye, matrix, NT, preferred_element_type=F32).astype(BF16)
+
+    def beside(blocks):
+        return jnp.concatenate(blocks, axis=1)
+
+    w1_rows[...] = jnp.zeros_like(w1_rows)
+    wl_rows[...] = jnp.zeros_like(wl_rows)
+    for a in range(3):
+        for b in range(3):
+            k = 3 * a + b
+            for c in range(3):
+                pair = w_first[k, c].astype(F32)
+                for m in range(2):
+                    at_row = a * 32 + b * 8 + c
+                    w1_rows[at_row : at_row + 1, m * HID : (m + 1) * HID] = pair[m : m + 1]
+            for m in range(2):
+                at_row = a * 24 + b * 8 + 4 + 2 * m
+                wl_rows[at_row : at_row + 2, m * HID : (m + 1) * HID] = w_last[m, k].astype(F32)
+    w1 = flip(w1_rows[...].astype(BF16))
+    wl = wl_rows[...].astype(BF16)
+    gap = jnp.zeros((8, 2 * HID), F32)
+    w3 = jnp.concatenate([p for t in (2, 1, 0) for p in (wl_rows[24 * t : 24 * t + 24, :], gap)], axis=0)
+    w3t = flip(w3.astype(BF16))
+    w2 = [
+        jnp.concatenate([beside([w_middle[m, 3 * a + b] for b in range(3)]) for a in range(3)], axis=0)
+        for m in range(2)
+    ]
+    w2t = [
+        flip(jnp.concatenate([beside([w_middle[m, 3 * a + b] for a in range(3)]) for b in range(3)], axis=0))
+        for m in range(2)
+    ]
 
     def arrived(kind, l, src, dst):
         pltpu.make_async_copy(src, dst, cr_sem.at[kind, l]).wait()
@@ -222,58 +268,48 @@
     def received(x):
         return jnp.concatenate([rx[l, x].astype(F32) for l in range(n_lon)], axis=-1)
 
-    def fill_s0(x, carry):
-        v = received(x)
-        s0[x] = jnp.concatenate(
-            [shift_cols(v, 1), v, shift_cols(v, -1), jnp.zeros_like(v)], axis=0
-        ).astype(BF16)
-        return carry
-
-    lax.fori_loop(0, rc + 2 * HALO, fill_s0, 0)
-
-    def first_layer(r, carry):
-        block = s0[pl.ds(r, 3)].reshape(96, width)
-        h = jnp.tanh(jnp.dot(w1[...], block, preferred_element_type=F32)) * inside(lat * rc - 4 + r)
+    def three(v):
+        return jnp.concatenate([shift_cols(v, 1), v, shift_cols(v, -1), jnp.zeros_like(v)], axis=0)
+
+    for x in range(rc + 2 * HALO):
+        s0[x] = three(received(x)).astype(BF16)
+
+    for r in range(rc + 8):
+        block = s0[r : r + 3].reshape(96, width)
+        h = jnp.tanh(jnp.dot(w1, block, preferred_element_type=F32)) * inside(lat * rc - 4 + r)
         for m in range(2):
             hm = h[m * HID : (m + 1) * HID]
             s1[m, r, 0:HID] = shift_cols(hm, 1).astype(BF16)
             s1[m, r, HID : 2 * HID] = hm.astype(BF16)
             s1[m, r, 2 * HID : 3 * HID] = shift_cols(hm, -1).astype(BF16)
-        return carry
-
-    lax.fori_loop(0, rc + 8, first_layer, 0)
-
-    def second_layer(r, carry):
-        keep = inside(lat * rc - 3 + r)
-        for m in range(2):
-            block = s1[m, pl.ds(r, 3)].reshape(9 * HID, width)
-            h = jnp.tanh(jnp.dot(w2[m], block, preferred_element_type=F32)) * keep
+
+    def taps(products, r, order):
+        return sum(
+            products[r + i][j * HID : (j + 1) * HID] for i, j in enumerate(order)
+        )
+
+    for m in range(2):
+        products = [
+            jnp.dot(w2[m], s1[m, x], preferred_element_type=F32) for x in range(rc + 8)
+        ]
+        for r in range(rc + 6):
+            h = jnp.tanh(taps(products, r, (0, 1, 2))) * inside(lat * rc - 3 + r)
             h2s[r, m * HID : (m + 1) * HID] = h.astype(BF16)
-        return carry
-
-    lax.fori_loop(0, rc + 6, second_layer, 0)
 
     scale = 2.0 / (2.0 * LEV * nyc * width)
     sub = lax.broadcasted_iota(jnp.int32, (8, width), 0)
-
-    def last_layer(r, carry):
-        block = h2s[pl.ds(r, 3)].reshape(6 * HID, width)
-        u = jnp.dot(wl[...], block, preferred_element_type=F32)
-        pred = shift_cols(u[0:8], 1) + u[8:16] + shift_cols(u[16:24], -1)
+    outs = [jnp.dot(wl, h2s[x], preferred_element_type=F32) for x in range(rc + 6)]
+    for r in range(rc + 4):
+        u = [sum(outs[r + a][24 * a + 8 * b : 24 * a + 8 * b + 8] for a in range(3)) for b in range(3)]
+        pred = shift_cols(u[0], 1) + u[1] + shift_cols(u[2], -1)
         g3 = jnp.where(sub >= 4, (pred - received(r + 3)) * scale, 0.0) * inside(lat * rc - 2 + r)
         g3s[r] = jnp.concatenate(
             [shift_cols(g3, -1), g3, shift_cols(g3, 1), jnp.zeros_like(g3)], axis=0
         ).astype(BF16)
-        both = pred[4:6] + pred[6:8]
-
-        @pl.when(jnp.logical_and(r >= 2, r < 2 + rc))
-        def _():
+        if 2 <= r < 2 + rc:
+            both = pred[4:6] + pred[6:8]
             for o in range(2):
-                pred_buf[o, pl.ds(r - 2, 1), :] = both[o : o + 1]
-
-        return carry
-
-    lax.fori_loop(0, rc + 4, last_layer, 0)
+                pred_buf[o, r - 2 : r - 1, :] = both[o : o + 1]
 
     def force_copy(l, m):
         return pltpu.make_async_remote_copy(
@@ -298,66 +334,80 @@
 
     force_own().start()
 
-    def back_second(r, carry):
-        block = g3s[pl.ds(r, 3)].reshape(96, width)
+    for r in range(rc + 2):
+        block = g3s[r : r + 3].reshape(96, width)
         h = h2s[r + 2].astype(F32)
-        d = jnp.dot(w3t[...], block, preferred_element_type=F32) * (1.0 - h * h)
+        d = jnp.dot(w3t, block, preferred_element_type=F32) * (1.0 - h * h)
         d = d * inside(lat * rc - 1 + r)
         for m in range(2):
             dm = d[m * HID : (m + 1) * HID]
             d2s[m, r, 0:HID] = shift_cols(dm, -1).astype(BF16)
             d2s[m, r, HID : 2 * HID] = dm.astype(BF16)
             d2s[m, r, 2 * HID : 3 * HID] = shift_cols(dm, 1).astype(BF16)
-        return carry
-
-    lax.fori_loop(0, rc + 2, back_second, 0)
-
-    def own_row(r, carry):
-        ups = g3s[pl.ds(r + 1, 3)].reshape(96, width)
-        acc_last[...] += lax.dot_general(ups, h2s[r + 3], NT, preferred_element_type=F32)
-        parts = []
-        for m in range(2):
-            hidden = s1[m, pl.ds(r + 3, 3), HID : 2 * HID]
-            acc_mid[m] += lax.dot_general(
-                d2s[m, r + 1], hidden.reshape(3 * HID, width), NT, preferred_element_type=F32
-            )
-            block = d2s[m, pl.ds(r, 3)].reshape(9 * HID, width)
+
+    def over_rows(left, right):
+        return lax.dot_general(
+            beside([left(r) for r in range(rc)]), beside([right(r) for r in range(rc)]), NT,
+            preferred_element_type=F32,
+        )
+
+    mids = [
+        over_rows(
+            lambda r: d2s[m, r + 1],
+            lambda r: s1[m, r + 3 : r + 6, HID : 2 * HID].reshape(3 * HID, width),
+        )
+        for m in range(2)
+    ]
+    for a in range(3):
+        partial[a * 192 : (a + 1) * 192, :] = beside(
+            [mids[m][:, a * HID : (a + 1) * HID] for m in range(2)]
+        )
+    last = over_rows(lambda r: g3s[r + 1 : r + 4].reshape(96, width), lambda r: h2s[r + 3])
+    for a in range(3):
+        at_row = MID_ROWS + 24 * a
+        partial[at_row : at_row + 24, :] = last[32 * a : 32 * a + 24, :]
+
+    def piece(ref, index):
+        return ref.at[pl.ds(pl.multiple_of(index * chunk, chunk), chunk)]
+
+    def scatter(low, high):
+        def send(i, carry):
+            to = low + lax.rem(me + i, high - low)
+
+            @pl.when(to != me)
+            def _():
+                pltpu.make_async_remote_copy(
+                    src_ref=piece(partial, to), dst_ref=scattered.at[me],
+                    send_sem=rs_send, recv_sem=rs_recv, device_id=of_group(to), device_id_type=MESH,
+                ).start()
+
+            return carry
+
+        lax.fori_loop(0, high - low, send, 0)
+
+    early = (MID_ROWS + SMALL_ROWS) // chunk
+    scatter(0, early)
+
+    d1s = []
+    for m in range(2):
+        products = [
+            jnp.dot(w2t[m], d2s[m, x], preferred_element_type=F32) for x in range(rc + 2)
+        ]
+        own = []
+        for r in range(rc):
             h = s1[m, r + 4, HID : 2 * HID].astype(F32)
-            d = jnp.dot(w2t[m], block, preferred_element_type=F32) * (1.0 - h * h)
-            parts.append(d.astype(BF16))
-        d1 = jnp.concatenate(parts, axis=0)
-        xs = s0[pl.ds(r + 4, 3)].reshape(96, width)
-        acc_first[...] += lax.dot_general(xs, d1, NT, preferred_element_type=F32)
-        return carry
-
-    lax.fori_loop(0, rc, own_row, 0)
-
+            own.append((taps(products, r, (2, 1, 0)) * (1.0 - h * h)).astype(BF16))
+        d1s.append(own)
+    first = over_rows(
+        lambda r: s0[r + 4 : r + 7].reshape(96, width),
+        lambda r: jnp.concatenate([d1s[0][r], d1s[1][r]], axis=0),
+    )
     for a in range(3):
-        partial[a * 192 : (a + 1) * 192, :] = jnp.concatenate(
-            [acc_mid[m, :, a * HID : (a + 1) * HID] for m in range(2)], axis=-1
-        )
-        partial[MID_ROWS + 24 * a : MID_ROWS + 24 * a + 24, :] = acc_first[32 * a : 32 * a + 24, :]
         at_row = MID_ROWS + SMALL_ROWS + 24 * a
-        partial[at_row : at_row + 24, :] = acc_last[32 * a : 32 * a + 24, :]
+        partial[at_row : at_row + 24, :] = first[32 * a : 32 * a + 24, :]
     if owners * chunk > GRAD_ROWS:
         partial[GRAD_ROWS:, :] = jnp.zeros((owners * chunk - GRAD_ROWS, 128), F32)
-
-    def piece(ref, index):
-        return ref.at[pl.ds(pl.multiple_of(index * chunk, chunk), chunk)]
-
-    def scatter(i, carry):
-        to = lax.rem(me + i, group)
-
-        @pl.when(to < owners)
-        def _():
-            pltpu.make_async_remote_copy(
-                src_ref=piece(partial, to), dst_ref=scattered.at[i - 1],
-                send_sem=rs_send, recv_sem=rs_recv, device_id=of_group(to), device_id_type=MESH,
-            ).start()
-
-        return carry
-
-    lax.fori_loop(1, group, scatter, 0)
+    scatter(early, owners)
 
     for m in range(n_mem):
         for l in range(n_lon):
@@ -393,6 +443,7 @@
         pad[q, 7:8, :] = row_rx[0, q : q + 1, :]
         pad[q, 8 + rows : 9 + rows, :] = row_rx[1, q : q + 1, :]
 
+    loads[4].wait()
     lane_ids = lax.broadcasted_iota(jnp.int32, (8, cols), 1)
     for s in range(rows // 8):
         base = 8 + 8 * s
@@ -421,16 +472,23 @@
             sum_y = sum_y + dy
             fu = force_up[l * 2, 8 * s : 8 * s + 8, :]
             fv = force_up[l * 2 + 1, 8 * s : 8 * s + 8, :]
-            velo_out[0, l, 8 * s : 8 * s + 8, :] = u + wet * (
+            velo_new[0, l, 8 * s : 8 * s + 8, :] = u + wet * (
                 coriolis * v + 0.25 * sum_x + 0.5 * laps[0] + fu
             )
-            velo_out[1, l, 8 * s : 8 * s + 8, :] = v + wet * (
+            velo_new[1, l, 8 * s : 8 * s + 8, :] = v + wet * (
                 -coriolis * u + 0.25 * sum_y + 0.5 * laps[1] + fv
             )
-            temp_out[l, 8 * s : 8 * s + 8, :] = t + wet * (
+            temp_new[l, 8 * s : 8 * s + 8, :] = t + wet * (
                 -0.5 * (u * dx + v * dy) + 0.3 * laps[2]
             )
 
+    stores = [
+        pltpu.make_async_copy(velo_new, velo_out, out_sem.at[0]),
+        pltpu.make_async_copy(temp_new, temp_out, out_sem.at[1]),
+    ]
+    for store in stores:
+        store.start()
+
     def passed(ref, count, sem):
         pltpu.make_async_copy(ref.at[pl.ds(0, count)], ref.at[pl.ds(0, count)], sem).wait()
 
@@ -439,11 +497,11 @@
         passed(scattered, group - 1, rs_recv)
 
         def add(i, total):
-            return total + scattered[i]
+            return total + scattered[lax.rem(me + i, group)]
 
         start = pl.multiple_of(me * chunk, chunk)
         grads[pl.ds(start, chunk), :] = lax.fori_loop(
-            0, group - 1, add, partial[pl.ds(start, chunk), :]
+            1, group, add, partial[pl.ds(start, chunk), :]
         )
 
         def gather(i, carry):
@@ -456,6 +514,8 @@
 
         lax.fori_loop(1, group, gather, 0)
 
+    for store in stores:
+        store.wait()
     for l in range(n_lon):
         @pl.when(lat < n_lat - 1)
         def _(l=l):
@@ -495,6 +555,28 @@
     def _():
         passed(partial, owners * chunk, rs_send)
         passed(grads, owners * chunk, ag_recv)
+
+
+def finish(velo_in, temp_in, grads, velo_out, temp_out, first, middle, last, sems):
+    moves = [
+        pltpu.make_async_copy(velo_in.at[c], velo_out.at[c], sems.at[c]) for c in range(2)
+    ]
+    moves.append(pltpu.make_async_copy(temp_in, temp_out, sems.at[2]))
+    for move in moves:
+        move.start()
+    for a in range(3):
+        for b in range(3):
+            k = 3 * a + b
+            for m in range(2):
+                cols = slice(m * HID, (m + 1) * HID)
+                middle[m, k] = grads[a * 192 + b * HID : a * 192 + (b + 1) * HID, cols]
+                at_row = MID_ROWS + (2 - a) * 24 + b * 8 + 4 + 2 * m
+                last[m, k] = grads[at_row : at_row + 2, cols]
+                for c in range(3):
+                    at_row = MID_ROWS + SMALL_ROWS + a * 24 + b * 8 + c
+                    first[k, c, m : m + 1, :] = grads[at_row : at_row + 1, cols]
+    for move in moves:
+        move.wait()
 
 
 def per_device(n_lat, n_lon, n_mem, velo, temp, land, target, w_first, w_middle, w_last):
@@ -505,34 +587,20 @@
     chunk, owners = chunking(group)
     mine = w_first.shape[0]
 
-    wf = w_first.reshape(mine, 3, 3, HID, 3)
-    wm = w_middle.reshape(mine, 3, 3, HID, HID)
-    wo = w_last.reshape(mine, 3, 3, 2, HID)
-    w1 = jnp.pad(jnp.transpose(wf, (0, 3, 1, 2, 4)), ((0, 0), (0, 0), (0, 0), (0, 1), (0, 5)))
-    w1 = w1.reshape(mine * HID, 96)
-    w2 = jnp.transpose(wm, (0, 3, 1, 2, 4)).reshape(mine, HID, 9 * HID)
-    w2t = jnp.transpose(wm[:, ::-1], (0, 4, 1, 2, 3)).reshape(mine, HID, 9 * HID)
-    eye = jnp.eye(mine, dtype=BF16)
-    wl = jnp.pad(
-        jnp.einsum("mabox,mn->bnoamx", wo, eye).reshape(3, 4, 6 * HID), ((0, 0), (4, 0), (0, 0))
-    ).reshape(24, 6 * HID)
-    w3t = jnp.pad(
-        jnp.einsum("mabox,mn->mxabno", wo[:, ::-1], eye).reshape(mine * HID, 3, 3, 4),
-        ((0, 0), (0, 0), (0, 1), (4, 0)),
-    ).reshape(mine * HID, 96)
-
     vmem = pl.BlockSpec(memory_space=pltpu.VMEM)
+    hbm = pl.BlockSpec(memory_space=pl.ANY)
     dma = pltpu.SemaphoreType.DMA
+    fields = [jax.ShapeDtypeStruct(velo.shape, F32), jax.ShapeDtypeStruct(temp.shape, F32)]
     velo_next, temp_next, grads = pl.pallas_call(
         functools.partial(kernel, n_lat, n_lon, n_mem),
-        out_shape=(
-            jax.ShapeDtypeStruct(velo.shape, F32),
-            jax.ShapeDtypeStruct(temp.shape, F32),
-            jax.ShapeDtypeStruct((owners * chunk, 128), F32),
-        ),
-        in_specs=[vmem] * 9,
-        out_specs=(vmem, vmem, vmem),
+        out_shape=(*fields, jax.ShapeDtypeStruct((owners * chunk, 128), F32)),
+        in_specs=[hbm] * 4 + [vmem] * 3,
+        out_specs=(hbm, hbm, vmem),
         scratch_shapes=[
+            pltpu.VMEM(velo.shape, F32),
+            pltpu.VMEM(temp.shape, F32),
+            pltpu.VMEM(land.shape, jnp.int32),
+            pltpu.VMEM(target.shape, BF16),
             pltpu.VMEM((LEV * rows, cc), F32),
             pltpu.VMEM((LEV * 2 * rows, cc), F32),
             pltpu.VMEM((LEV * rc * 8, cc), F32),
@@ -551,11 +619,12 @@
             pltpu.VMEM((2, 16, cols), F32),
             pltpu.VMEM((2, rows, 128), F32),
             pltpu.VMEM((2, rows, 128), F32),
-            pltpu.VMEM((2, 3 * HID, 3 * HID), F32),
             pltpu.VMEM((96, 128), F32),
-            pltpu.VMEM((96, 128), F32),
+            pltpu.VMEM((72, 128), F32),
             pltpu.VMEM((owners * chunk, 128), F32),
-            pltpu.VMEM((group - 1, chunk, 128), F32),
+            pltpu.VMEM((group, chunk, 128), F32),
+            dma((5,)),
+            dma((2,)),
             dma((3, n_lon)),
             dma((3, n_lon)),
             dma((4,)),
@@ -572,16 +641,21 @@
             collective_id=0, has_side_effects=True, vmem_limit_bytes=56 * 1024 * 1024
         ),
         name="ocean_step",
-    )(velo, temp, land, target, w1, w2, w2t, wl, w3t)
-
-    mid = grads[:MID_ROWS].reshape(3, 3, HID, mine, HID)
-    grad_middle = jnp.transpose(mid, (3, 0, 1, 2, 4)).reshape(mine, 9, HID, HID)
-    first = grads[MID_ROWS : MID_ROWS + SMALL_ROWS].reshape(9, 8, mine, HID)[:, :3]
-    grad_first = jnp.transpose(first, (2, 0, 3, 1))
-    last = grads[MID_ROWS + SMALL_ROWS : GRAD_ROWS].reshape(3, 3, 8, mine, HID)[::-1, :, 4:]
-    last = last.reshape(9, mine, 2, mine, HID)
-    grad_last = jnp.stack([last[:, m, :, m] for m in range(mine)], 0)
-    return (velo_next, temp_next, grad_first, grad_middle, grad_last)
+    )(velo, temp, land, target, jnp.transpose(w_first, (1, 3, 0, 2)), w_middle, w_last)
+    velo_next, temp_next, first, middle, last = pl.pallas_call(
+        finish,
+        out_shape=(
+            *fields,
+            jax.ShapeDtypeStruct((9, 3, mine, HID), F32),
+            jax.ShapeDtypeStruct(w_middle.shape, F32),
+            jax.ShapeDtypeStruct(w_last.shape, F32),
+        ),
+        in_specs=[hbm, hbm, vmem],
+        out_specs=(hbm, hbm, vmem, vmem, vmem),
+        scratch_shapes=[dma((3,))],
+        name="finish",
+    )(velo_next, temp_next, grads)
+    return (velo_next, temp_next, jnp.transpose(first, (2, 0, 3, 1)), middle, last)
 
 
 def solution(mesh):

time: 70.3 us -> 67 us (0.953)
  local copies, waits for them, and re-layouts: 11.8 us -> 0 us
  Pallas kernels: 56.7 us -> 66.2 us
  other arithmetic: 0.72 us -> 0 us
    pallas_call x0 -> x1, Pallas kernels: none -> 26.8 us  [per_device(): pl.pallas_call(finish, out_shape=(*fields, jax.ShapeDtypeStruct((9, 3, mi...]
    pallas_call x1, Pallas kernels: 56.7 us -> 39.4 us  [per_device(): pl.pallas_call(functools.partial(kernel, n_lat, n_lon, n_mem), out_shape=...]
    reshape x12 -> x0, local copies, waits for them, and re-layouts: 5.25 us -> none  [the longest x1 0.84 us: per_device(): w2 = jnp.transpose(wm, (0, 3, 1, 2, 4)).reshape(mine, HID, 9 * HID)]
    unnamed x10 -> x0, local copies, waits for them, and re-layouts: 2.2 us -> none
    slice x4 -> x0, local copies, waits for them, and re-layouts: 1.8 us -> none  [the longest x1 0.98 us: per_device(): mid = grads[:MID_ROWS].reshape(3, 3, HID, mine, HID)]
    transpose x4 -> x0, local copies, waits for them, and re-layouts: 1.71 us -> none  [the longest x1 0.88 us: per_device(): grad_middle = jnp.transpose(mid, (3, 0, 1, 2, 4)).reshape(mine, 9, HID, HID)]
    rev x4 -> x0, local copies, waits for them, and re-layouts: 0.78 us -> none  [the longest x2 0.76 us: per_device(): wo[:, ::-1]]
where the time goes in v2:
time: 67 us; the launch traced here: 66.8 us
  Pallas kernels  66.2 us (99%)
    pallas_call x1, Pallas kernels, per_device(): pl.pallas_call(functools.partial(kernel, n_lat, n_lon, n_mem), out_shape=...  39.4 us
    pallas_call x1, Pallas kernels, per_device(): pl.pallas_call(finish, out_shape=(*fields, jax.ShapeDtypeStruct((9, 3, mi...  26.8 us

profile of v2, /device:TPU:1, one launch (start us, length us, event | category | flops | bytes accessed | tf_op | source)
XLA Modules:
  0.0 66.8 jit_solution(2999594457473856729)
XLA Ops:
  0.6 39.4 %ocean_step.1 = (f32[2,4,32,512]{3,2,1,0:T(8,128)}, f32[4,32,512]{2,1,0:T(8,128)}, f32[720,128]{1,0:T(8,128)}) custom-call(f32[2,4,32,512]{3,2,1,0:T(8,128)} %velo_in.1, f32[4,32,512]{2,1,0:T(8,128)} %temp_in.1, s32[32,512]{1,0:T(8,128)} %land_in.1, bf16[2,4,8,128]{3,2,1,0:T(8,128)(2,1)} %target_in.1, bf16[9,3,2,64]{3,2,1,0:T(2,128)(2,1)} %bitcast.2, ...), custom_call_target="tpu_custom_call" | custom-call | tf_op jit(solution)/shard_map/ocean_step/pallas_call | solution.py:594
  40.1 26.8 %finish.1 = (f32[2,4,32,512]{3,2,1,0:T(8,128)}, f32[4,32,512]{2,1,0:T(8,128)}, f32[9,3,2,64]{3,2,1,0:T(2,128)}, f32[2,9,64,64]{3,2,1,0:T(8,128)}, f32[2,9,2,64]{3,2,1,0:T(2,128)}) custom-call(f32[2,4,32,512]{3,2,1,0:T(8,128)} %get-tuple-element.13.velo_in, f32[4,32,512]{2,1,0:T(8,128)} %get-tuple-element.14.temp_in, f32[720,128]{1,0:T(8,128)} %get-tuple-element.15.grads), custom_call_target="tpu_custom_call" | custom-call | tf_op jit(solution)/shard_map/finish/pallas_call | solution.py:645

commit v3 on v2

--- a/solution.py
+++ b/solution.py
@@ -21,9 +21,9 @@
 NT = (((1,), (1,)), ((), ()))
 
 
-def chunking(group):
-    tiles = GRAD_ROWS // 8
-    per = -(-tiles // group)
+def chunking(plane):
+    tiles = -(-GRAD_ROWS // 16)
+    per = -(-tiles // plane)
     owners = -(-tiles // per)
     return per * 8, owners
 
@@ -38,9 +38,9 @@
     velo_out, temp_out, grads,
     velo_new, temp_new, land, target,
     narrow, tall, staged, send_buf, rx, s0, s1, h2s, g3s, d2s, pred_buf, force_rx, force_up, pad,
-    row_send, row_rx, col_send, col_rx, w1_rows, wl_rows, partial, scattered,
+    row_send, row_rx, col_send, col_rx, w1_rows, wl_rows, partial, theirs, halved, scattered, gathered,
     in_sem, out_sem,
-    cs_sem, cr_sem, os_sem, or_sem, fs_sem, fr_sem, fl_sem, rs_send, rs_recv, ag_send, ag_recv,
+    cp_send, cp_recv, cs_sem, cr_sem, os_sem, or_sem, fs_sem, fr_sem, fl_sem, rs_send, rs_recv, ag_send, ag_recv,
 ):
     lat = lax.axis_index("lat")
     lon = lax.axis_index("lon")
@@ -52,8 +52,14 @@
     width = cc * n_lon
     nyc = rc * n_lat
     group = n_lat * n_lon
-    chunk, owners = chunking(group)
+    planes = n_lon // 2
+    plane = n_lat * planes
+    chunk, owners = chunking(plane)
+    half = chunk * owners
+    core = lax.rem(lon, 2)
+    partner = lon + 1 - 2 * core
     me = lat * n_lon + lon
+    rank = lat * planes + lon // 2
 
     def at(lat_to, lon_to, mem_to):
         return {"lat": lat_to, "lon": lon_to, "mem": mem_to}
@@ -73,6 +79,9 @@
     loads.append(pltpu.make_async_copy(land_in, land, in_sem.at[4]))
     for load in loads:
         load.start()
+
+    def of_plane(index):
+        return at(index // planes, 2 * lax.rem(index, planes) + core, mem)
 
     barrier = pltpu.get_barrier_semaphore()
 
@@ -358,35 +367,30 @@
         )
         for m in range(2)
     ]
+    def put(start, value):
+        low = min(max(half - start, 0), value.shape[0])
+        if low > 0:
+            partial[0, start : start + low, :] = value[:low]
+        if low < value.shape[0]:
+            partial[1, start + low - half : start + value.shape[0] - half, :] = value[low:]
+
     for a in range(3):
-        partial[a * 192 : (a + 1) * 192, :] = beside(
-            [mids[m][:, a * HID : (a + 1) * HID] for m in range(2)]
-        )
+        put(a * 192, beside([mids[m][:, a * HID : (a + 1) * HID] for m in range(2)]))
     last = over_rows(lambda r: g3s[r + 1 : r + 4].reshape(96, width), lambda r: h2s[r + 3])
     for a in range(3):
         at_row = MID_ROWS + 24 * a
-        partial[at_row : at_row + 24, :] = last[32 * a : 32 * a + 24, :]
-
-    def piece(ref, index):
-        return ref.at[pl.ds(pl.multiple_of(index * chunk, chunk), chunk)]
-
-    def scatter(low, high):
-        def send(i, carry):
-            to = low + lax.rem(me + i, high - low)
-
-            @pl.when(to != me)
-            def _():
-                pltpu.make_async_remote_copy(
-                    src_ref=piece(partial, to), dst_ref=scattered.at[me],
-                    send_sem=rs_send, recv_sem=rs_recv, device_id=of_group(to), device_id_type=MESH,
-                ).start()
-
-            return carry
-
-        lax.fori_loop(0, high - low, send, 0)
-
-    early = (MID_ROWS + SMALL_ROWS) // chunk
-    scatter(0, early)
+        put(at_row, last[32 * a : 32 * a + 24, :])
+
+    def core_copy(which):
+        start, size = ((0, split), (split, half - split))[which]
+        return pltpu.make_async_remote_copy(
+            src_ref=partial.at[1 - core, pl.ds(start, size)], dst_ref=theirs.at[pl.ds(start, size)],
+            send_sem=cp_send.at[which], recv_sem=cp_recv.at[which],
+            device_id=at(lat, partner, mem), device_id_type=MESH,
+        )
+
+    split = (MID_ROWS + SMALL_ROWS - half) // 8 * 8
+    core_copy(0).start()
 
     d1s = []
     for m in range(2):
@@ -404,10 +408,27 @@
     )
     for a in range(3):
         at_row = MID_ROWS + SMALL_ROWS + 24 * a
-        partial[at_row : at_row + 24, :] = first[32 * a : 32 * a + 24, :]
-    if owners * chunk > GRAD_ROWS:
-        partial[GRAD_ROWS:, :] = jnp.zeros((owners * chunk - GRAD_ROWS, 128), F32)
-    scatter(early, owners)
+        put(at_row, first[32 * a : 32 * a + 24, :])
+    if 2 * half > GRAD_ROWS:
+        put(GRAD_ROWS, jnp.zeros((2 * half - GRAD_ROWS, 128), F32))
+    core_copy(1).start()
+    for which in range(2):
+        core_copy(which).wait()
+    halved[...] = partial[core] + theirs[...]
+
+    def piece(ref, index):
+        return ref.at[pl.ds(pl.multiple_of(index * chunk, chunk), chunk)]
+
+    for i in range(owners):
+        to = lax.rem(rank + i, owners)
+
+        @pl.when(to != rank)
+        def _(to=to):
+            pltpu.make_async_remote_copy(
+                src_ref=piece(halved, to), dst_ref=scattered.at[rank],
+                send_sem=rs_send, recv_sem=rs_recv, device_id=of_plane(to), device_id_type=MESH,
+            ).start()
+
 
     for m in range(n_mem):
         for l in range(n_lon):
@@ -492,27 +513,35 @@
     def passed(ref, count, sem):
         pltpu.make_async_copy(ref.at[pl.ds(0, count)], ref.at[pl.ds(0, count)], sem).wait()
 
-    @pl.when(me < owners)
-    def _():
-        passed(scattered, group - 1, rs_recv)
-
-        def add(i, total):
-            return total + scattered[lax.rem(me + i, group)]
-
-        start = pl.multiple_of(me * chunk, chunk)
-        grads[pl.ds(start, chunk), :] = lax.fori_loop(
-            1, group, add, partial[pl.ds(start, chunk), :]
-        )
-
-        def gather(i, carry):
+    @pl.when(rank < owners)
+    def _():
+        passed(scattered, plane - 1, rs_recv)
+        start = pl.multiple_of(rank * chunk, chunk)
+        total = halved[pl.ds(start, chunk), :]
+        for i in range(1, plane):
+            total = total + scattered[lax.rem(rank + i, plane)]
+        gathered[core, pl.ds(start, chunk), :] = total
+        for i in range(1, plane):
             pltpu.make_async_remote_copy(
-                src_ref=piece(grads, me), dst_ref=piece(grads, me),
+                src_ref=piece(gathered.at[core], rank), dst_ref=piece(gathered.at[core], rank),
                 send_sem=ag_send, recv_sem=ag_recv,
-                device_id=of_group(lax.rem(me + i, group)), device_id_type=MESH,
+                device_id=of_plane(lax.rem(rank + i, plane)), device_id_type=MESH,
             ).start()
-            return carry
-
-        lax.fori_loop(1, group, gather, 0)
+
+    @pl.when(rank < owners)
+    def _():
+        passed(halved, (owners - 1) * chunk, ag_recv)
+
+    @pl.when(rank >= owners)
+    def _():
+        passed(halved, owners * chunk, ag_recv)
+
+    share = pltpu.make_async_remote_copy(
+        src_ref=gathered.at[core], dst_ref=gathered.at[core],
+        send_sem=cp_send.at[2], recv_sem=cp_recv.at[2],
+        device_id=at(lat, partner, mem), device_id_type=MESH,
+    )
+    share.start()
 
     for store in stores:
         store.wait()
@@ -545,46 +574,62 @@
     col_east().wait_send()
     col_west().wait_send()
 
-    @pl.when(me < owners)
-    def _():
-        passed(partial, (owners - 1) * chunk, rs_send)
-        passed(grads, (owners - 1) * chunk, ag_recv)
-        passed(scattered, group - 1, ag_send)
-
-    @pl.when(me >= owners)
-    def _():
-        passed(partial, owners * chunk, rs_send)
-        passed(grads, owners * chunk, ag_recv)
-
-
-def finish(velo_in, temp_in, grads, velo_out, temp_out, first, middle, last, sems):
-    moves = [
-        pltpu.make_async_copy(velo_in.at[c], velo_out.at[c], sems.at[c]) for c in range(2)
-    ]
-    moves.append(pltpu.make_async_copy(temp_in, temp_out, sems.at[2]))
-    for move in moves:
-        move.start()
+    @pl.when(rank < owners)
+    def _():
+        passed(halved, (owners - 1) * chunk, rs_send)
+        passed(scattered, plane - 1, ag_send)
+
+    @pl.when(rank >= owners)
+    def _():
+        passed(halved, owners * chunk, rs_send)
+
+    share.wait()
+    grads[...] = gathered[...]
+
+
+def finish(velo_in, temp_in, halves, velo_out, temp_out, first, middle, last, velo, temp, sems):
+    blocks = [(velo_in.at[c], velo.at[c], velo_out.at[c]) for c in range(2)]
+    blocks.append((temp_in, temp, temp_out))
+    loads = [pltpu.make_async_copy(b[0], b[1], sems.at[i]) for i, b in enumerate(blocks)]
+    stores = [pltpu.make_async_copy(b[1], b[2], sems.at[i]) for i, b in enumerate(blocks)]
+    for load in loads:
+        load.start()
+    for load, store in zip(loads, stores):
+        load.wait()
+        store.start()
+    half = halves.shape[1]
+
+    def rows_of(start, size, cols):
+        low = min(max(half - start, 0), size)
+        parts = []
+        if low > 0:
+            parts.append(halves[0, start : start + low, cols])
+        if low < size:
+            parts.append(halves[1, start + low - half : start + size - half, cols])
+        return parts[0] if len(parts) == 1 else jnp.concatenate(parts, axis=0)
+
     for a in range(3):
         for b in range(3):
             k = 3 * a + b
             for m in range(2):
                 cols = slice(m * HID, (m + 1) * HID)
-                middle[m, k] = grads[a * 192 + b * HID : a * 192 + (b + 1) * HID, cols]
+                middle[m, k] = rows_of(a * 192 + b * HID, HID, cols)
                 at_row = MID_ROWS + (2 - a) * 24 + b * 8 + 4 + 2 * m
-                last[m, k] = grads[at_row : at_row + 2, cols]
+                last[m, k] = rows_of(at_row, 2, cols)
                 for c in range(3):
                     at_row = MID_ROWS + SMALL_ROWS + a * 24 + b * 8 + c
-                    first[k, c, m : m + 1, :] = grads[at_row : at_row + 1, cols]
-    for move in moves:
-        move.wait()
+                    first[k, c, m : m + 1, :] = rows_of(at_row, 1, cols)
+    for store in stores:
+        store.wait()
 
 
 def per_device(n_lat, n_lon, n_mem, velo, temp, land, target, w_first, w_middle, w_last):
     rows, cols = temp.shape[1], temp.shape[2]
     rc, cc = rows // COARSE, cols // COARSE
     width = cc * n_lon
-    group = n_lat * n_lon
-    chunk, owners = chunking(group)
+    plane = n_lat * (n_lon // 2)
+    chunk, owners = chunking(plane)
+    half = chunk * owners
     mine = w_first.shape[0]
 
     vmem = pl.BlockSpec(memory_space=pltpu.VMEM)
@@ -593,7 +638,7 @@
     fields = [jax.ShapeDtypeStruct(velo.shape, F32), jax.ShapeDtypeStruct(temp.shape, F32)]
     velo_next, temp_next, grads = pl.pallas_call(
         functools.partial(kernel, n_lat, n_lon, n_mem),
-        out_shape=(*fields, jax.ShapeDtypeStruct((owners * chunk, 128), F32)),
+        out_shape=(*fields, jax.ShapeDtypeStruct((2, half, 128), F32)),
         in_specs=[hbm] * 4 + [vmem] * 3,
         out_specs=(hbm, hbm, vmem),
         scratch_shapes=[
@@ -621,10 +666,15 @@
             pltpu.VMEM((2, rows, 128), F32),
             pltpu.VMEM((96, 128), F32),
             pltpu.VMEM((72, 128), F32),
-            pltpu.VMEM((owners * chunk, 128), F32),
-            pltpu.VMEM((group, chunk, 128), F32),
+            pltpu.VMEM((2, half, 128), F32),
+            pltpu.VMEM((half, 128), F32),
+            pltpu.VMEM((half, 128), F32),
+            pltpu.VMEM((plane, chunk, 128), F32),
+            pltpu.VMEM((2, half, 128), F32),
             dma((5,)),
             dma((2,)),
+            dma((3,)),
+            dma((3,)),
             dma((3, n_lon)),
             dma((3, n_lon)),
             dma((4,)),
@@ -652,7 +702,7 @@
         ),
         in_specs=[hbm, hbm, vmem],
         out_specs=(hbm, hbm, vmem, vmem, vmem),
-        scratch_shapes=[dma((3,))],
+        scratch_shapes=[pltpu.VMEM(velo.shape, F32), pltpu.VMEM(temp.shape, F32), dma((3,))],
         name="finish",
     )(velo_next, temp_next, grads)
     return (velo_next, temp_next, jnp.transpose(first, (2, 0, 3, 1)), middle, last)

time: 67 us -> 41.7 us (0.62)
  Pallas kernels: 66.2 us -> 40.8 us
    pallas_call x1, Pallas kernels: 26.8 us -> 3.65 us  [per_device(): pl.pallas_call(finish, out_shape=(*fields, jax.ShapeDtypeStruct((9, 3, mi...]
    pallas_call x1, Pallas kernels: 39.4 us -> 37.2 us  [per_device(): pl.pallas_call(functools.partial(kernel, n_lat, n_lon, n_mem), out_shape=...]
where the time goes in v3:
time: 41.7 us; the launch traced here: 41.5 us
  Pallas kernels  40.8 us (98%)
  between operations  0.64 us (2%)
    pallas_call x1, Pallas kernels, per_device(): pl.pallas_call(functools.partial(kernel, n_lat, n_lon, n_mem), out_shape=...  37.2 us
    pallas_call x1, Pallas kernels, per_device(): pl.pallas_call(finish, out_shape=(*fields, jax.ShapeDtypeStruct((9, 3, mi...  3.65 us

profile of v3, /device:TPU:1, one launch (start us, length us, event | category | flops | bytes accessed | tf_op | source)
XLA Modules:
  0.0 41.5 jit_solution(11194416031166743438)
XLA Ops:
  0.6 37.2 %ocean_step.1 = (f32[2,4,32,512]{3,2,1,0:T(8,128)}, f32[4,32,512]{2,1,0:T(8,128)}, f32[2,368,128]{2,1,0:T(8,128)}) custom-call(f32[2,4,32,512]{3,2,1,0:T(8,128)} %velo_in.1, f32[4,32,512]{2,1,0:T(8,128)} %temp_in.1, s32[32,512]{1,0:T(8,128)} %land_in.1, bf16[2,4,8,128]{3,2,1,0:T(8,128)(2,1)} %target_in.1, bf16[9,3,2,64]{3,2,1,0:T(2,128)(2,1)} %bitcast.2, ...), custom_call_target="tpu_custom_call" | custom-call | tf_op jit(solution)/shard_map/ocean_step/pallas_call | solution.py:639
  37.8 3.7 %finish.1 = (f32[2,4,32,512]{3,2,1,0:T(8,128)}, f32[4,32,512]{2,1,0:T(8,128)}, f32[9,3,2,64]{3,2,1,0:T(2,128)}, f32[2,9,64,64]{3,2,1,0:T(8,128)}, f32[2,9,2,64]{3,2,1,0:T(2,128)}) custom-call(f32[2,4,32,512]{3,2,1,0:T(8,128)} %get-tuple-element.13.velo_in, f32[4,32,512]{2,1,0:T(8,128)} %get-tuple-element.14.temp_in, f32[2,368,128]{2,1,0:T(8,128)} %get-tuple-element.15.halves), custom_call_target="tpu_custom_call" | custom-call | tf_op jit(solution)/shard_map/finish/pallas_call | solution.py:695

commit v4 on v3

--- a/solution.py
+++ b/solution.py
@@ -28,15 +28,29 @@
     return per * 8, owners
 
 
+EARLY = (MID_ROWS + SMALL_ROWS) // 8
+LOW_EARLY, LOW_LATE = (EARLY + 1) // 2, (SMALL_ROWS // 8 + 1) // 2
+
+
+def place(tile):
+    if tile < EARLY:
+        return divmod_half(tile, LOW_EARLY, 0, 0)
+    return divmod_half(tile - EARLY, LOW_LATE, LOW_EARLY, EARLY - LOW_EARLY)
+
+
+def divmod_half(tile, low, base_low, base_high):
+    return (0, 8 * (base_low + tile)) if tile < low else (1, 8 * (base_high + tile - low))
+
+
 def shift_cols(value, by):
     return pltpu.roll(value, by % value.shape[-1], axis=value.ndim - 1)
 
 
 def kernel(
     n_lat, n_lon, n_mem,
-    velo_in, temp_in, land_in, target_in, w_first, w_middle, w_last,
+    velo_in, temp_in, land_in, target_in, first_in, middle_in, last_in,
     velo_out, temp_out, grads,
-    velo_new, temp_new, land, target,
+    velo_new, temp_new, land, target, w_first, w_middle, w_last,
     narrow, tall, staged, send_buf, rx, s0, s1, h2s, g3s, d2s, pred_buf, force_rx, force_up, pad,
     row_send, row_rx, col_send, col_rx, w1_rows, wl_rows, partial, theirs, halved, scattered, gathered,
     in_sem, out_sem,
@@ -61,6 +75,12 @@
     me = lat * n_lon + lon
     rank = lat * planes + lon // 2
 
+    def owner(turn_of):
+        return (turn_of * plane) // owners
+
+    turn = (rank * owners + plane - 1) // plane
+    is_owner = jnp.logical_and(turn < owners, owner(turn) == rank)
+
     def at(lat_to, lon_to, mem_to):
         return {"lat": lat_to, "lon": lon_to, "mem": mem_to}
 
@@ -77,6 +97,9 @@
     )
     loads.append(pltpu.make_async_copy(target_in, target, in_sem.at[3]))
     loads.append(pltpu.make_async_copy(land_in, land, in_sem.at[4]))
+    loads.append(pltpu.make_async_copy(first_in, w_first, in_sem.at[5]))
+    loads.append(pltpu.make_async_copy(middle_in, w_middle, in_sem.at[6]))
+    loads.append(pltpu.make_async_copy(last_in, w_last, in_sem.at[7]))
     for load in loads:
         load.start()
 
@@ -107,10 +130,17 @@
     staged[...] = jnp.zeros_like(staged)
     for c in range(3):
         fine = pad[c * LEV : (c + 1) * LEV, 8 : 8 + rows, :].reshape(LEV * rows, cols)
-        narrow[...] = lax.dot_general(
-            fine * (1.0 / COARSE**2), expand, NT,
-            precision=lax.Precision.HIGHEST, preferred_element_type=F32,
-        )
+        fine = fine * (1.0 / COARSE**2)
+        high = fine.astype(BF16)
+        rest = fine - high.astype(F32)
+        middle = rest.astype(BF16)
+        low = (rest - middle.astype(F32)).astype(BF16)
+        parts = lax.dot_general(
+            jnp.concatenate([high, middle, low], axis=0), expand.astype(BF16), NT,
+            preferred_element_type=F32,
+        )
+        n = LEV * rows
+        narrow[...] = parts[0:n] + parts[n : 2 * n] + parts[2 * n : 3 * n]
         pooled = narrow[pl.ds(0, LEV * rc, stride=COARSE), :]
         for r in range(1, COARSE):
             pooled = pooled + narrow[pl.ds(r, LEV * rc, stride=COARSE), :]
@@ -120,6 +150,76 @@
         staged[pl.ds(4 + c, LEV * rc, stride=8), :] = goal
         staged[pl.ds(6 + c, LEV * rc, stride=8), :] = goal
     send_buf[...] = staged[...].astype(BF16).reshape(send_buf.shape)
+
+    @pl.when(lat == 0)
+    def _():
+        rx[:, 0:HALO] = jnp.zeros((n_lon, HALO, 8, cc), BF16)
+        row_rx[0] = jnp.zeros_like(row_rx[0])
+
+    @pl.when(lat == n_lat - 1)
+    def _():
+        rx[:, HALO + rc : 2 * HALO + rc] = jnp.zeros((n_lon, HALO, 8, cc), BF16)
+        row_rx[1] = jnp.zeros_like(row_rx[1])
+
+    pl.semaphore_wait(barrier, group - 1 + (n_mem - 1) * n_lon)
+
+    def own_copy(l):
+        return pltpu.make_async_remote_copy(
+            src_ref=send_buf.at[l], dst_ref=rx.at[lon, pl.ds(HALO, rc)],
+            send_sem=cs_sem.at[0, l], recv_sem=cr_sem.at[0, lon],
+            device_id=at(lat, l, mem), device_id_type=MESH,
+        )
+
+    def up_copy(l):
+        return pltpu.make_async_remote_copy(
+            src_ref=send_buf.at[l, pl.ds(rc - HALO, HALO)], dst_ref=rx.at[lon, pl.ds(0, HALO)],
+            send_sem=cs_sem.at[1, l], recv_sem=cr_sem.at[1, lon],
+            device_id=at(lat + 1, l, mem), device_id_type=MESH,
+        )
+
+    def down_copy(l):
+        return pltpu.make_async_remote_copy(
+            src_ref=send_buf.at[l, pl.ds(0, HALO)], dst_ref=rx.at[lon, pl.ds(HALO + rc, HALO)],
+            send_sem=cs_sem.at[2, l], recv_sem=cr_sem.at[2, lon],
+            device_id=at(lat - 1, l, mem), device_id_type=MESH,
+        )
+
+    def row_up():
+        return pltpu.make_async_remote_copy(
+            src_ref=row_send.at[1], dst_ref=row_rx.at[0], send_sem=os_sem.at[0], recv_sem=or_sem.at[0],
+            device_id=at(lat + 1, lon, mem), device_id_type=MESH,
+        )
+
+    def row_down():
+        return pltpu.make_async_remote_copy(
+            src_ref=row_send.at[0], dst_ref=row_rx.at[1], send_sem=os_sem.at[1], recv_sem=or_sem.at[1],
+            device_id=at(lat - 1, lon, mem), device_id_type=MESH,
+        )
+
+    def col_east():
+        return pltpu.make_async_remote_copy(
+            src_ref=col_send.at[1], dst_ref=col_rx.at[0], send_sem=os_sem.at[2], recv_sem=or_sem.at[2],
+            device_id=at(lat, lax.rem(lon + 1, n_lon), mem), device_id_type=MESH,
+        )
+
+    def col_west():
+        return pltpu.make_async_remote_copy(
+            src_ref=col_send.at[0], dst_ref=col_rx.at[1], send_sem=os_sem.at[3], recv_sem=or_sem.at[3],
+            device_id=at(lat, lax.rem(lon + n_lon - 1, n_lon), mem), device_id_type=MESH,
+        )
+
+    for l in range(n_lon):
+        @pl.when(lat < n_lat - 1)
+        def _(l=l):
+            up_copy(l).start()
+
+        @pl.when(lat > 0)
+        def _(l=l):
+            down_copy(l).start()
+
+        @pl.when(lon != l)
+        def _(l=l):
+            own_copy(l).start()
 
     lane = lax.broadcasted_iota(jnp.int32, (rows, 128), 1)
     west_cols = jnp.zeros((rows, 128), F32)
@@ -134,76 +234,6 @@
     col_send[0] = west_cols
     col_send[1] = east_cols
 
-    @pl.when(lat == 0)
-    def _():
-        rx[:, 0:HALO] = jnp.zeros((n_lon, HALO, 8, cc), BF16)
-        row_rx[0] = jnp.zeros_like(row_rx[0])
-
-    @pl.when(lat == n_lat - 1)
-    def _():
-        rx[:, HALO + rc : 2 * HALO + rc] = jnp.zeros((n_lon, HALO, 8, cc), BF16)
-        row_rx[1] = jnp.zeros_like(row_rx[1])
-
-    pl.semaphore_wait(barrier, group - 1 + (n_mem - 1) * n_lon)
-
-    def own_copy(l):
-        return pltpu.make_async_remote_copy(
-            src_ref=send_buf.at[l], dst_ref=rx.at[lon, pl.ds(HALO, rc)],
-            send_sem=cs_sem.at[0, l], recv_sem=cr_sem.at[0, lon],
-            device_id=at(lat, l, mem), device_id_type=MESH,
-        )
-
-    def up_copy(l):
-        return pltpu.make_async_remote_copy(
-            src_ref=send_buf.at[l, pl.ds(rc - HALO, HALO)], dst_ref=rx.at[lon, pl.ds(0, HALO)],
-            send_sem=cs_sem.at[1, l], recv_sem=cr_sem.at[1, lon],
-            device_id=at(lat + 1, l, mem), device_id_type=MESH,
-        )
-
-    def down_copy(l):
-        return pltpu.make_async_remote_copy(
-            src_ref=send_buf.at[l, pl.ds(0, HALO)], dst_ref=rx.at[lon, pl.ds(HALO + rc, HALO)],
-            send_sem=cs_sem.at[2, l], recv_sem=cr_sem.at[2, lon],
-            device_id=at(lat - 1, l, mem), device_id_type=MESH,
-        )
-
-    def row_up():
-        return pltpu.make_async_remote_copy(
-            src_ref=row_send.at[1], dst_ref=row_rx.at[0], send_sem=os_sem.at[0], recv_sem=or_sem.at[0],
-            device_id=at(lat + 1, lon, mem), device_id_type=MESH,
-        )
-
-    def row_down():
-        return pltpu.make_async_remote_copy(
-            src_ref=row_send.at[0], dst_ref=row_rx.at[1], send_sem=os_sem.at[1], recv_sem=or_sem.at[1],
-            device_id=at(lat - 1, lon, mem), device_id_type=MESH,
-        )
-
-    def col_east():
-        return pltpu.make_async_remote_copy(
-            src_ref=col_send.at[1], dst_ref=col_rx.at[0], send_sem=os_sem.at[2], recv_sem=or_sem.at[2],
-            device_id=at(lat, lax.rem(lon + 1, n_lon), mem), device_id_type=MESH,
-        )
-
-    def col_west():
-        return pltpu.make_async_remote_copy(
-            src_ref=col_send.at[0], dst_ref=col_rx.at[1], send_sem=os_sem.at[3], recv_sem=or_sem.at[3],
-            device_id=at(lat, lax.rem(lon + n_lon - 1, n_lon), mem), device_id_type=MESH,
-        )
-
-    for l in range(n_lon):
-        @pl.when(lat < n_lat - 1)
-        def _(l=l):
-            up_copy(l).start()
-
-        @pl.when(lat > 0)
-        def _(l=l):
-            down_copy(l).start()
-
-        @pl.when(lon != l)
-        def _(l=l):
-            own_copy(l).start()
-
     @pl.when(lat < n_lat - 1)
     def _():
         row_up().start()
@@ -228,6 +258,8 @@
     def beside(blocks):
         return jnp.concatenate(blocks, axis=1)
 
+    for load in loads[5:]:
+        load.wait()
     w1_rows[...] = jnp.zeros_like(w1_rows)
     wl_rows[...] = jnp.zeros_like(wl_rows)
     for a in range(3):
@@ -368,11 +400,9 @@
         for m in range(2)
     ]
     def put(start, value):
-        low = min(max(half - start, 0), value.shape[0])
-        if low > 0:
-            partial[0, start : start + low, :] = value[:low]
-        if low < value.shape[0]:
-            partial[1, start + low - half : start + value.shape[0] - half, :] = value[low:]
+        for i in range(value.shape[0] // 8):
+            side, row = place(start // 8 + i)
+            partial[side, row : row + 8, :] = value[8 * i : 8 * i + 8]
 
     for a in range(3):
         put(a * 192, beside([mids[m][:, a * HID : (a + 1) * HID] for m in range(2)]))
@@ -389,8 +419,28 @@
             device_id=at(lat, partner, mem), device_id_type=MESH,
         )
 
-    split = (MID_ROWS + SMALL_ROWS - half) // 8 * 8
+    early = 8 * (EARLY - LOW_EARLY) // chunk
+    split = early * chunk
     core_copy(0).start()
+
+    def piece(ref, index):
+        return ref.at[pl.ds(pl.multiple_of(index * chunk, chunk), chunk)]
+
+    def reduce_rows(which):
+        core_copy(which).wait()
+        start, count = ((0, early), (early, owners - early))[which]
+        span = slice(start * chunk, (start + count) * chunk)
+        halved[span, :] = partial[core, span, :] + theirs[span, :]
+        for i in range(count):
+            to = start + lax.rem(rank + i, count)
+
+            @pl.when(owner(to) != rank)
+            def _(to=to):
+                pltpu.make_async_remote_copy(
+                    src_ref=piece(halved, to), dst_ref=scattered.at[rank],
+                    send_sem=rs_send, recv_sem=rs_recv,
+                    device_id=of_plane(owner(to)), device_id_type=MESH,
+                ).start()
 
     d1s = []
     for m in range(2):
@@ -402,6 +452,8 @@
             h = s1[m, r + 4, HID : 2 * HID].astype(F32)
             own.append((taps(products, r, (2, 1, 0)) * (1.0 - h * h)).astype(BF16))
         d1s.append(own)
+        if m == 0:
+            reduce_rows(0)
     first = over_rows(
         lambda r: s0[r + 4 : r + 7].reshape(96, width),
         lambda r: jnp.concatenate([d1s[0][r], d1s[1][r]], axis=0),
@@ -409,26 +461,11 @@
     for a in range(3):
         at_row = MID_ROWS + SMALL_ROWS + 24 * a
         put(at_row, first[32 * a : 32 * a + 24, :])
-    if 2 * half > GRAD_ROWS:
-        put(GRAD_ROWS, jnp.zeros((2 * half - GRAD_ROWS, 128), F32))
+    used = 8 * (EARLY - LOW_EARLY + SMALL_ROWS // 8 - LOW_LATE)
+    if half > used:
+        partial[1, used:, :] = jnp.zeros((half - used, 128), F32)
     core_copy(1).start()
-    for which in range(2):
-        core_copy(which).wait()
-    halved[...] = partial[core] + theirs[...]
-
-    def piece(ref, index):
-        return ref.at[pl.ds(pl.multiple_of(index * chunk, chunk), chunk)]
-
-    for i in range(owners):
-        to = lax.rem(rank + i, owners)
-
-        @pl.when(to != rank)
-        def _(to=to):
-            pltpu.make_async_remote_copy(
-                src_ref=piece(halved, to), dst_ref=scattered.at[rank],
-                send_sem=rs_send, recv_sem=rs_recv, device_id=of_plane(to), device_id_type=MESH,
-            ).start()
-
+    reduce_rows(1)
 
     for m in range(n_mem):
         for l in range(n_lon):
@@ -513,26 +550,26 @@
     def passed(ref, count, sem):
         pltpu.make_async_copy(ref.at[pl.ds(0, count)], ref.at[pl.ds(0, count)], sem).wait()
 
-    @pl.when(rank < owners)
+    @pl.when(is_owner)
     def _():
         passed(scattered, plane - 1, rs_recv)
-        start = pl.multiple_of(rank * chunk, chunk)
+        start = pl.multiple_of(turn * chunk, chunk)
         total = halved[pl.ds(start, chunk), :]
         for i in range(1, plane):
             total = total + scattered[lax.rem(rank + i, plane)]
         gathered[core, pl.ds(start, chunk), :] = total
         for i in range(1, plane):
             pltpu.make_async_remote_copy(
-                src_ref=piece(gathered.at[core], rank), dst_ref=piece(gathered.at[core], rank),
+                src_ref=piece(gathered.at[core], turn), dst_ref=piece(gathered.at[core], turn),
                 send_sem=ag_send, recv_sem=ag_recv,
                 device_id=of_plane(lax.rem(rank + i, plane)), device_id_type=MESH,
             ).start()
 
-    @pl.when(rank < owners)
+    @pl.when(is_owner)
     def _():
         passed(halved, (owners - 1) * chunk, ag_recv)
 
-    @pl.when(rank >= owners)
+    @pl.when(jnp.logical_not(is_owner))
     def _():
         passed(halved, owners * chunk, ag_recv)
 
@@ -542,6 +579,8 @@
         device_id=at(lat, partner, mem), device_id_type=MESH,
     )
     share.start()
+    keep = pltpu.make_async_copy(gathered.at[core], grads.at[core], out_sem.at[2])
+    keep.start()
 
     for store in stores:
         store.wait()
@@ -574,51 +613,62 @@
     col_east().wait_send()
     col_west().wait_send()
 
-    @pl.when(rank < owners)
+    @pl.when(is_owner)
     def _():
         passed(halved, (owners - 1) * chunk, rs_send)
         passed(scattered, plane - 1, ag_send)
 
-    @pl.when(rank >= owners)
+    @pl.when(jnp.logical_not(is_owner))
     def _():
         passed(halved, owners * chunk, rs_send)
 
     share.wait()
-    grads[...] = gathered[...]
-
-
-def finish(velo_in, temp_in, halves, velo_out, temp_out, first, middle, last, velo, temp, sems):
+    fetched = pltpu.make_async_copy(gathered.at[1 - core], grads.at[1 - core], out_sem.at[3])
+    fetched.start()
+    keep.wait()
+    fetched.wait()
+
+
+def finish(
+    velo_in, temp_in, halves_in, velo_out, temp_out, first_out, middle_out, last_out,
+    velo, temp, halves, first, middle, last, sems,
+):
+    load = pltpu.make_async_copy(halves_in, halves, sems.at[0])
+    load.start()
     blocks = [(velo_in.at[c], velo.at[c], velo_out.at[c]) for c in range(2)]
     blocks.append((temp_in, temp, temp_out))
-    loads = [pltpu.make_async_copy(b[0], b[1], sems.at[i]) for i, b in enumerate(blocks)]
-    stores = [pltpu.make_async_copy(b[1], b[2], sems.at[i]) for i, b in enumerate(blocks)]
-    for load in loads:
-        load.start()
-    for load, store in zip(loads, stores):
-        load.wait()
-        store.start()
-    half = halves.shape[1]
+    moves = [pltpu.make_async_copy(b[0], b[1], sems.at[1 + i]) for i, b in enumerate(blocks)]
+    for move in moves:
+        move.start()
+    load.wait()
 
     def rows_of(start, size, cols):
-        low = min(max(half - start, 0), size)
-        parts = []
-        if low > 0:
-            parts.append(halves[0, start : start + low, cols])
-        if low < size:
-            parts.append(halves[1, start + low - half : start + size - half, cols])
-        return parts[0] if len(parts) == 1 else jnp.concatenate(parts, axis=0)
-
-    for a in range(3):
-        for b in range(3):
-            k = 3 * a + b
-            for m in range(2):
-                cols = slice(m * HID, (m + 1) * HID)
-                middle[m, k] = rows_of(a * 192 + b * HID, HID, cols)
+        side, row = place(start // 8)
+        return halves[side, row + start % 8 : row + start % 8 + size, cols]
+
+    stores = []
+    for m in range(2):
+        cols = slice(m * HID, (m + 1) * HID)
+        for a in range(3):
+            for b in range(3):
+                k = 3 * a + b
+                for i in range(HID // 8):
+                    middle[m, k, 8 * i : 8 * i + 8] = rows_of(a * 192 + b * HID + 8 * i, 8, cols)
                 at_row = MID_ROWS + (2 - a) * 24 + b * 8 + 4 + 2 * m
                 last[m, k] = rows_of(at_row, 2, cols)
                 for c in range(3):
                     at_row = MID_ROWS + SMALL_ROWS + a * 24 + b * 8 + c
                     first[k, c, m : m + 1, :] = rows_of(at_row, 1, cols)
+        stores.append(pltpu.make_async_copy(middle.at[m], middle_out.at[m], sems.at[4 + m]))
+        stores[-1].start()
+    stores.append(pltpu.make_async_copy(first, first_out, sems.at[6]))
+    stores.append(pltpu.make_async_copy(last, last_out, sems.at[7]))
+    for store in stores[2:]:
+        store.start()
+    for i, (move, b) in enumerate(zip(moves, blocks)):
+        move.wait()
+        stores.append(pltpu.make_async_copy(b[1], b[2], sems.at[8 + i]))
+        stores[-1].start()
     for store in stores:
         store.wait()
 
@@ -632,20 +682,22 @@
     half = chunk * owners
     mine = w_first.shape[0]
 
-    vmem = pl.BlockSpec(memory_space=pltpu.VMEM)
     hbm = pl.BlockSpec(memory_space=pl.ANY)
     dma = pltpu.SemaphoreType.DMA
     fields = [jax.ShapeDtypeStruct(velo.shape, F32), jax.ShapeDtypeStruct(temp.shape, F32)]
     velo_next, temp_next, grads = pl.pallas_call(
         functools.partial(kernel, n_lat, n_lon, n_mem),
         out_shape=(*fields, jax.ShapeDtypeStruct((2, half, 128), F32)),
-        in_specs=[hbm] * 4 + [vmem] * 3,
-        out_specs=(hbm, hbm, vmem),
+        in_specs=[hbm] * 7,
+        out_specs=(hbm, hbm, hbm),
         scratch_shapes=[
             pltpu.VMEM(velo.shape, F32),
             pltpu.VMEM(temp.shape, F32),
             pltpu.VMEM(land.shape, jnp.int32),
             pltpu.VMEM(target.shape, BF16),
+            pltpu.VMEM((9, 3, mine, HID), BF16),
+            pltpu.VMEM(w_middle.shape, BF16),
+            pltpu.VMEM(w_last.shape, BF16),
             pltpu.VMEM((LEV * rows, cc), F32),
             pltpu.VMEM((LEV * 2 * rows, cc), F32),
             pltpu.VMEM((LEV * rc * 8, cc), F32),
@@ -671,8 +723,8 @@
             pltpu.VMEM((half, 128), F32),
             pltpu.VMEM((plane, chunk, 128), F32),
             pltpu.VMEM((2, half, 128), F32),
-            dma((5,)),
-            dma((2,)),
+            dma((8,)),
+            dma((4,)),
             dma((3,)),
             dma((3,)),
             dma((3, n_lon)),
@@ -700,9 +752,17 @@
             jax.ShapeDtypeStruct(w_middle.shape, F32),
             jax.ShapeDtypeStruct(w_last.shape, F32),
         ),
-        in_specs=[hbm, hbm, vmem],
-        out_specs=(hbm, hbm, vmem, vmem, vmem),
-        scratch_shapes=[pltpu.VMEM(velo.shape, F32), pltpu.VMEM(temp.shape, F32), dma((3,))],
+        in_specs=[hbm] * 3,
+        out_specs=(hbm,) * 5,
+        scratch_shapes=[
+            pltpu.VMEM(velo.shape, F32),
+            pltpu.VMEM(temp.shape, F32),
+            pltpu.VMEM((2, half, 128), F32),
+            pltpu.VMEM((9, 3, mine, HID), F32),
+            pltpu.VMEM(w_middle.shape, F32),
+            pltpu.VMEM(w_last.shape, F32),
+            dma((11,)),
+        ],
         name="finish",
     )(velo_next, temp_next, grads)
     return (velo_next, temp_next, jnp.transpose(first, (2, 0, 3, 1)), middle, last)

time: 41.7 us -> 38.2 us (0.916)
  Pallas kernels: 40.8 us -> 37.4 us
    pallas_call x1, Pallas kernels: 37.2 us -> 35.2 us  [per_device(): pl.pallas_call(functools.partial(kernel, n_lat, n_lon, n_mem), out_shape=...]
    pallas_call x1, Pallas kernels: 3.65 us -> 2.24 us  [per_device(): pl.pallas_call(finish, out_shape=(*fields, jax.ShapeDtypeStruct((9, 3, mi...]
where the time goes in v4:
time: 38.2 us; the launch traced here: 38.1 us
  Pallas kernels  37.4 us (98%)
  between operations  0.64 us (2%)
    pallas_call x1, Pallas kernels, per_device(): pl.pallas_call(functools.partial(kernel, n_lat, n_lon, n_mem), out_shape=...  35.2 us
    pallas_call x1, Pallas kernels, per_device(): pl.pallas_call(finish, out_shape=(*fields, jax.ShapeDtypeStruct((9, 3, mi...  2.24 us

profile of v4, /device:TPU:1, one launch (start us, length us, event | category | flops | bytes accessed | tf_op | source)
XLA Modules:
  0.0 38.1 jit_solution(14420619690105768743)
XLA Ops:
  0.6 35.2 %ocean_step.1 = (f32[2,4,32,512]{3,2,1,0:T(8,128)}, f32[4,32,512]{2,1,0:T(8,128)}, f32[2,368,128]{2,1,0:T(8,128)}) custom-call(f32[2,4,32,512]{3,2,1,0:T(8,128)} %velo_in.1, f32[4,32,512]{2,1,0:T(8,128)} %temp_in.1, s32[32,512]{1,0:T(8,128)} %land_in.1, bf16[2,4,8,128]{3,2,1,0:T(8,128)(2,1)} %target_in.1, bf16[9,3,2,64]{3,2,1,0:T(2,128)(2,1)} %bitcast.2, ...), custom_call_target="tpu_custom_call" | custom-call | tf_op jit(solution)/shard_map/ocean_step/pallas_call | solution.py:688
  35.8 2.2 %finish.1 = (f32[2,4,32,512]{3,2,1,0:T(8,128)}, f32[4,32,512]{2,1,0:T(8,128)}, f32[9,3,2,64]{3,2,1,0:T(2,128)}, f32[2,9,64,64]{3,2,1,0:T(8,128)}, f32[2,9,2,64]{3,2,1,0:T(2,128)}) custom-call(f32[2,4,32,512]{3,2,1,0:T(8,128)} %get-tuple-element.13.velo_in, f32[4,32,512]{2,1,0:T(8,128)} %get-tuple-element.14.temp_in, f32[2,368,128]{2,1,0:T(8,128)} %get-tuple-element.15.halves_in), custom_call_target="tpu_custom_call" | custom-call | tf_op jit(solution)/shard_map/finish/pallas_call | solution.py:747

commit v5 on v4

--- a/solution.py
+++ b/solution.py
@@ -21,11 +21,10 @@
 NT = (((1,), (1,)), ((), ()))
 
 
-def chunking(plane):
+def chunking(n_lat, planes):
     tiles = -(-GRAD_ROWS // 16)
-    per = -(-tiles // plane)
-    owners = -(-tiles // per)
-    return per * 8, owners
+    owners = (n_lat // 4 * 3 if n_lat % 4 == 0 else n_lat) * planes
+    return -(-tiles // owners) * 8, owners
 
 
 EARLY = (MID_ROWS + SMALL_ROWS) // 8
@@ -68,18 +67,32 @@
     group = n_lat * n_lon
     planes = n_lon // 2
     plane = n_lat * planes
-    chunk, owners = chunking(plane)
+    chunk, owners = chunking(n_lat, planes)
     half = chunk * owners
     core = lax.rem(lon, 2)
     partner = lon + 1 - 2 * core
     me = lat * n_lon + lon
-    rank = lat * planes + lon // 2
-
-    def owner(turn_of):
-        return (turn_of * plane) // owners
-
-    turn = (rank * owners + plane - 1) // plane
-    is_owner = jnp.logical_and(turn < owners, owner(turn) == rank)
+    place_z = lax.div(lon, 2)
+    rank = lat * planes + place_z
+
+    def owns(lat_of):
+        return lax.rem(lat_of, 4) != 3 if n_lat % 4 == 0 else lat_of >= 0
+
+    def turn_of(lat_of, z_of):
+        return (lat_of - lax.div(lat_of, 4) if n_lat % 4 == 0 else lat_of) * planes + z_of
+
+    turn = turn_of(lat, place_z)
+    is_owner = owns(lat)
+
+    def wrapped(value, size):
+        return jnp.where(value >= size, value - size, value)
+
+    def around(which):
+        for i in list(range(1, n_lat)) + [0]:
+            for k in range(planes):
+                z = wrapped(place_z + (k + 1 if i == 0 else k), planes)
+                if i > 0 or k < planes - 1:
+                    which(wrapped(lat + i, n_lat), z)
 
     def at(lat_to, lon_to, mem_to):
         return {"lat": lat_to, "lon": lon_to, "mem": mem_to}
@@ -103,8 +116,8 @@
     for load in loads:
         load.start()
 
-    def of_plane(index):
-        return at(index // planes, 2 * lax.rem(index, planes) + core, mem)
+    def of_plane(lat_to, z_to):
+        return at(lat_to, 2 * z_to + core, mem)
 
     barrier = pltpu.get_barrier_semaphore()
 
@@ -431,16 +444,20 @@
         start, count = ((0, early), (early, owners - early))[which]
         span = slice(start * chunk, (start + count) * chunk)
         halved[span, :] = partial[core, span, :] + theirs[span, :]
-        for i in range(count):
-            to = start + lax.rem(rank + i, count)
-
-            @pl.when(owner(to) != rank)
-            def _(to=to):
+
+        def send(lat_to, z_to):
+            to = turn_of(lat_to, z_to)
+            wanted = jnp.logical_and(to >= start, to < start + count)
+
+            @pl.when(jnp.logical_and(owns(lat_to), wanted))
+            def _():
                 pltpu.make_async_remote_copy(
                     src_ref=piece(halved, to), dst_ref=scattered.at[rank],
                     send_sem=rs_send, recv_sem=rs_recv,
-                    device_id=of_plane(owner(to)), device_id_type=MESH,
+                    device_id=of_plane(lat_to, z_to), device_id_type=MESH,
                 ).start()
+
+        around(send)
 
     d1s = []
     for m in range(2):
@@ -466,6 +483,33 @@
         partial[1, used:, :] = jnp.zeros((half - used, 128), F32)
     core_copy(1).start()
     reduce_rows(1)
+
+    def passed(ref, count, sem):
+        pltpu.make_async_copy(ref.at[pl.ds(0, count)], ref.at[pl.ds(0, count)], sem).wait()
+
+    @pl.when(is_owner)
+    def _():
+        passed(scattered, plane - 1, rs_recv)
+        start = pl.multiple_of(turn * chunk, chunk)
+        total = halved[pl.ds(start, chunk), :]
+        for i in range(1, plane):
+            total = total + scattered[lax.rem(rank + i, plane)]
+        gathered[core, pl.ds(start, chunk), :] = total
+
+        def spread(lat_to, z_to, sem):
+            pltpu.make_async_remote_copy(
+                src_ref=piece(gathered.at[core], turn), dst_ref=piece(gathered.at[core], turn),
+                send_sem=ag_send, recv_sem=ag_recv.at[sem],
+                device_id=of_plane(lat_to, z_to), device_id_type=MESH,
+            ).start()
+
+        @pl.when(turn < early)
+        def _():
+            around(functools.partial(spread, sem=0))
+
+        @pl.when(turn >= early)
+        def _():
+            around(functools.partial(spread, sem=1))
 
     for m in range(n_mem):
         for l in range(n_lon):
@@ -547,38 +591,28 @@
     for store in stores:
         store.start()
 
-    def passed(ref, count, sem):
-        pltpu.make_async_copy(ref.at[pl.ds(0, count)], ref.at[pl.ds(0, count)], sem).wait()
-
-    @pl.when(is_owner)
-    def _():
-        passed(scattered, plane - 1, rs_recv)
-        start = pl.multiple_of(turn * chunk, chunk)
-        total = halved[pl.ds(start, chunk), :]
-        for i in range(1, plane):
-            total = total + scattered[lax.rem(rank + i, plane)]
-        gathered[core, pl.ds(start, chunk), :] = total
-        for i in range(1, plane):
-            pltpu.make_async_remote_copy(
-                src_ref=piece(gathered.at[core], turn), dst_ref=piece(gathered.at[core], turn),
-                send_sem=ag_send, recv_sem=ag_recv,
-                device_id=of_plane(lax.rem(rank + i, plane)), device_id_type=MESH,
-            ).start()
-
-    @pl.when(is_owner)
-    def _():
-        passed(halved, (owners - 1) * chunk, ag_recv)
-
-    @pl.when(jnp.logical_not(is_owner))
-    def _():
-        passed(halved, owners * chunk, ag_recv)
-
-    share = pltpu.make_async_remote_copy(
-        src_ref=gathered.at[core], dst_ref=gathered.at[core],
-        send_sem=cp_send.at[2], recv_sem=cp_recv.at[2],
-        device_id=at(lat, partner, mem), device_id_type=MESH,
-    )
-    share.start()
+    def share(which):
+        start, count = ((0, early), (early, owners - early))[which]
+        span = pl.ds(start * chunk, count * chunk)
+        inside_it = jnp.logical_and(is_owner, jnp.logical_and(turn >= start, turn < start + count))
+        if count > 1:
+            @pl.when(inside_it)
+            def _():
+                passed(halved, (count - 1) * chunk, ag_recv.at[which])
+
+        @pl.when(jnp.logical_not(inside_it))
+        def _():
+            passed(halved, count * chunk, ag_recv.at[which])
+
+        copy = pltpu.make_async_remote_copy(
+            src_ref=gathered.at[core, span], dst_ref=gathered.at[core, span],
+            send_sem=cp_send.at[2 + which], recv_sem=cp_recv.at[2 + which],
+            device_id=at(lat, partner, mem), device_id_type=MESH,
+        )
+        copy.start()
+        return copy, span
+
+    shares = [share(0), share(1)]
     keep = pltpu.make_async_copy(gathered.at[core], grads.at[core], out_sem.at[2])
     keep.start()
 
@@ -622,11 +656,18 @@
     def _():
         passed(halved, owners * chunk, rs_send)
 
-    share.wait()
-    fetched = pltpu.make_async_copy(gathered.at[1 - core], grads.at[1 - core], out_sem.at[3])
-    fetched.start()
+    fetched = []
+    for which, (copy, span) in enumerate(shares):
+        copy.wait()
+        fetched.append(
+            pltpu.make_async_copy(
+                gathered.at[1 - core, span], grads.at[1 - core, span], out_sem.at[3 + which]
+            )
+        )
+        fetched[-1].start()
     keep.wait()
-    fetched.wait()
+    for fetch in fetched:
+        fetch.wait()
 
 
 def finish(
@@ -678,7 +719,7 @@
     rc, cc = rows // COARSE, cols // COARSE
     width = cc * n_lon
     plane = n_lat * (n_lon // 2)
-    chunk, owners = chunking(plane)
+    chunk, owners = chunking(n_lat, n_lon // 2)
     half = chunk * owners
     mine = w_first.shape[0]
 
@@ -724,9 +765,9 @@
             pltpu.VMEM((plane, chunk, 128), F32),
             pltpu.VMEM((2, half, 128), F32),
             dma((8,)),
+            dma((5,)),
             dma((4,)),
-            dma((3,)),
-            dma((3,)),
+            dma((4,)),
             dma((3, n_lon)),
             dma((3, n_lon)),
             dma((4,)),
@@ -737,7 +778,7 @@
             dma,
             dma,
             dma,
-            dma,
+            dma((2,)),
         ],
         compiler_params=pltpu.CompilerParams(
             collective_id=0, has_side_effects=True, vmem_limit_bytes=56 * 1024 * 1024

time: 38.2 us -> 38.8 us (1.016)
  Pallas kernels: 37.4 us -> 38 us
    pallas_call x1, Pallas kernels: 35.2 us -> 35.7 us  [per_device(): pl.pallas_call(functools.partial(kernel, n_lat, n_lon, n_mem), out_shape=...]
where the time goes in v5:
time: 38.8 us; the launch traced here: 38.6 us
  Pallas kernels  38 us (98%)
  between operations  0.64 us (2%)
    pallas_call x1, Pallas kernels, per_device(): pl.pallas_call(functools.partial(kernel, n_lat, n_lon, n_mem), out_shape=...  35.7 us
    pallas_call x1, Pallas kernels, per_device(): pl.pallas_call(finish, out_shape=(*fields, jax.ShapeDtypeStruct((9, 3, mi...  2.25 us

profile of v5, /device:TPU:1, one launch (start us, length us, event | category | flops | bytes accessed | tf_op | source)
XLA Modules:
  0.0 38.6 jit_solution(1640318712004262177)
XLA Ops:
  0.6 35.7 %ocean_step.1 = (f32[2,4,32,512]{3,2,1,0:T(8,128)}, f32[4,32,512]{2,1,0:T(8,128)}, f32[2,384,128]{2,1,0:T(8,128)}) custom-call(f32[2,4,32,512]{3,2,1,0:T(8,128)} %velo_in.1, f32[4,32,512]{2,1,0:T(8,128)} %temp_in.1, s32[32,512]{1,0:T(8,128)} %land_in.1, bf16[2,4,8,128]{3,2,1,0:T(8,128)(2,1)} %target_in.1, bf16[9,3,2,64]{3,2,1,0:T(2,128)(2,1)} %bitcast.2, ...), custom_call_target="tpu_custom_call" | custom-call | tf_op jit(solution)/shard_map/ocean_step/pallas_call | solution.py:729
  36.4 2.2 %finish.1 = (f32[2,4,32,512]{3,2,1,0:T(8,128)}, f32[4,32,512]{2,1,0:T(8,128)}, f32[9,3,2,64]{3,2,1,0:T(2,128)}, f32[2,9,64,64]{3,2,1,0:T(8,128)}, f32[2,9,2,64]{3,2,1,0:T(2,128)}) custom-call(f32[2,4,32,512]{3,2,1,0:T(8,128)} %get-tuple-element.13.velo_in, f32[4,32,512]{2,1,0:T(8,128)} %get-tuple-element.14.temp_in, f32[2,384,128]{2,1,0:T(8,128)} %get-tuple-element.15.halves_in), custom_call_target="tpu_custom_call" | custom-call | tf_op jit(solution)/shard_map/finish/pallas_call | solution.py:788

commit v6 on v5

--- a/solution.py
+++ b/solution.py
@@ -53,7 +53,7 @@
     narrow, tall, staged, send_buf, rx, s0, s1, h2s, g3s, d2s, pred_buf, force_rx, force_up, pad,
     row_send, row_rx, col_send, col_rx, w1_rows, wl_rows, partial, theirs, halved, scattered, gathered,
     in_sem, out_sem,
-    cp_send, cp_recv, cs_sem, cr_sem, os_sem, or_sem, fs_sem, fr_sem, fl_sem, rs_send, rs_recv, ag_send, ag_recv,
+    entered, cp_send, cp_recv, cs_sem, cr_sem, os_sem, or_sem, fs_sem, fr_sem, fl_sem, rs_send, rs_recv, ag_send, ag_recv,
 ):
     lat = lax.axis_index("lat")
     lon = lax.axis_index("lon")
@@ -64,14 +64,12 @@
     cc = cols // COARSE
     width = cc * n_lon
     nyc = rc * n_lat
-    group = n_lat * n_lon
     planes = n_lon // 2
     plane = n_lat * planes
     chunk, owners = chunking(n_lat, planes)
     half = chunk * owners
     core = lax.rem(lon, 2)
     partner = lon + 1 - 2 * core
-    me = lat * n_lon + lon
     place_z = lax.div(lon, 2)
     rank = lat * planes + place_z
 
@@ -96,9 +94,6 @@
 
     def at(lat_to, lon_to, mem_to):
         return {"lat": lat_to, "lon": lon_to, "mem": mem_to}
-
-    def of_group(index):
-        return at(index // n_lon, lax.rem(index, n_lon), mem)
 
     inner = pl.ds(8, rows)
     loads = [
@@ -121,27 +116,47 @@
 
     barrier = pltpu.get_barrier_semaphore()
 
-    def greet(i, carry):
-        pl.semaphore_signal(
-            barrier, inc=1, device_id=of_group(lax.rem(me + i, group)), device_id_type=MESH
-        )
-        return carry
-
-    lax.fori_loop(1, group, greet, 0)
-    for other in range(1, n_mem):
+    def greet(device):
+        pl.semaphore_signal(barrier, inc=1, device_id=device, device_id_type=MESH)
+
+    line = 4 if n_lat % 4 == 0 else n_lat
+    line_start = lax.div(lat, line) * line
+    greeted = 0
+    for i in range(line, n_lat, line):
+        for z in range(planes):
+            greet(of_plane(wrapped(lat + i, n_lat), z))
+            greeted += 1
+    for i in range(1, line):
+        for z in range(planes):
+            greet(of_plane(line_start + wrapped(lat - line_start + i, line), z))
+            greeted += 1
+    for i in range(1, n_lon):
+        greet(at(lat, wrapped(lon + i, n_lon), mem))
+        greeted += 1
+    for i in range(1, n_mem):
         for l in range(n_lon):
-            pl.semaphore_signal(
-                barrier, inc=1, device_id=at(lat, l, lax.rem(mem + other, n_mem)), device_id_type=MESH
-            )
+            greet(at(lat, l, wrapped(mem + i, n_mem)))
+            greeted += 1
+
+    @pl.when(lat > 0)
+    def _():
+        for l in range(n_lon):
+            greet(at(lat - 1, l, mem))
+
+    @pl.when(lat < n_lat - 1)
+    def _():
+        for l in range(n_lon):
+            greet(at(lat + 1, l, mem))
+
+    greeted = greeted + jnp.where(lat > 0, n_lon, 0) + jnp.where(lat < n_lat - 1, n_lon, 0)
 
     q_ids = lax.broadcasted_iota(jnp.int32, (cc, cols), 0)
     i_ids = lax.broadcasted_iota(jnp.int32, (cc, cols), 1)
     expand = jnp.where(i_ids // COARSE == q_ids, 1.0, 0.0).astype(F32)
 
-    for load in loads[:4]:
-        load.wait()
     staged[...] = jnp.zeros_like(staged)
     for c in range(3):
+        loads[c].wait()
         fine = pad[c * LEV : (c + 1) * LEV, 8 : 8 + rows, :].reshape(LEV * rows, cols)
         fine = fine * (1.0 / COARSE**2)
         high = fine.astype(BF16)
@@ -158,6 +173,7 @@
         for r in range(1, COARSE):
             pooled = pooled + narrow[pl.ds(r, LEV * rc, stride=COARSE), :]
         staged[pl.ds(c, LEV * rc, stride=8), :] = pooled
+    loads[3].wait()
     for c in range(2):
         goal = target[c].astype(F32).reshape(LEV * rc, cc)
         staged[pl.ds(4 + c, LEV * rc, stride=8), :] = goal
@@ -174,7 +190,7 @@
         rx[:, HALO + rc : 2 * HALO + rc] = jnp.zeros((n_lon, HALO, 8, cc), BF16)
         row_rx[1] = jnp.zeros_like(row_rx[1])
 
-    pl.semaphore_wait(barrier, group - 1 + (n_mem - 1) * n_lon)
+    pl.semaphore_wait(barrier, greeted)
 
     def own_copy(l):
         return pltpu.make_async_remote_copy(
@@ -233,6 +249,13 @@
         @pl.when(lon != l)
         def _(l=l):
             own_copy(l).start()
+
+    for i in range(1, line):
+        pl.semaphore_signal(
+            entered, inc=1,
+            device_id=of_plane(line_start + wrapped(lat - line_start + i, line), place_z),
+            device_id_type=MESH,
+        )
 
     lane = lax.broadcasted_iota(jnp.int32, (rows, 128), 1)
     west_cols = jnp.zeros((rows, 128), F32)
@@ -435,6 +458,8 @@
     early = 8 * (EARLY - LOW_EARLY) // chunk
     split = early * chunk
     core_copy(0).start()
+    if line > 1:
+        pl.semaphore_wait(entered, line - 1)
 
     def piece(ref, index):
         return ref.at[pl.ds(pl.multiple_of(index * chunk, chunk), chunk)]
@@ -766,6 +791,7 @@
             pltpu.VMEM((2, half, 128), F32),
             dma((8,)),
             dma((5,)),
+            pltpu.SemaphoreType.REGULAR,
             dma((4,)),
             dma((4,)),
             dma((3, n_lon)),

time: 38.8 us -> 37.4 us (0.964)
  Pallas kernels: 38 us -> 36.6 us
    pallas_call x1, Pallas kernels: 35.7 us -> 34.3 us  [per_device(): pl.pallas_call(functools.partial(kernel, n_lat, n_lon, n_mem), out_shape=...]
where the time goes in v6:
time: 37.4 us; the launch traced here: 37.2 us
  Pallas kernels  36.6 us (98%)
  between operations  0.64 us (2%)
    pallas_call x1, Pallas kernels, per_device(): pl.pallas_call(functools.partial(kernel, n_lat, n_lon, n_mem), out_shape=...  34.3 us
    pallas_call x1, Pallas kernels, per_device(): pl.pallas_call(finish, out_shape=(*fields, jax.ShapeDtypeStruct((9, 3, mi...  2.25 us

profile of v6, /device:TPU:1, one launch (start us, length us, event | category | flops | bytes accessed | tf_op | source)
XLA Modules:
  0.0 37.2 jit_solution(8382379486293071614)
XLA Ops:
  0.6 34.3 %ocean_step.1 = (f32[2,4,32,512]{3,2,1,0:T(8,128)}, f32[4,32,512]{2,1,0:T(8,128)}, f32[2,384,128]{2,1,0:T(8,128)}) custom-call(f32[2,4,32,512]{3,2,1,0:T(8,128)} %velo_in.1, f32[4,32,512]{2,1,0:T(8,128)} %temp_in.1, s32[32,512]{1,0:T(8,128)} %land_in.1, bf16[2,4,8,128]{3,2,1,0:T(8,128)(2,1)} %target_in.1, bf16[9,3,2,64]{3,2,1,0:T(2,128)(2,1)} %bitcast.2, ...), custom_call_target="tpu_custom_call" | custom-call | tf_op jit(solution)/shard_map/ocean_step/pallas_call | solution.py:754
  35.0 2.2 %finish.1 = (f32[2,4,32,512]{3,2,1,0:T(8,128)}, f32[4,32,512]{2,1,0:T(8,128)}, f32[9,3,2,64]{3,2,1,0:T(2,128)}, f32[2,9,64,64]{3,2,1,0:T(8,128)}, f32[2,9,2,64]{3,2,1,0:T(2,128)}) custom-call(f32[2,4,32,512]{3,2,1,0:T(8,128)} %get-tuple-element.13.velo_in, f32[4,32,512]{2,1,0:T(8,128)} %get-tuple-element.14.temp_in, f32[2,384,128]{2,1,0:T(8,128)} %get-tuple-element.15.halves_in), custom_call_target="tpu_custom_call" | custom-call | tf_op jit(solution)/shard_map/finish/pallas_call | solution.py:814

commit v7 on v6

--- a/solution.py
+++ b/solution.py
@@ -123,12 +123,12 @@
     line_start = lax.div(lat, line) * line
     greeted = 0
     for i in range(line, n_lat, line):
-        for z in range(planes):
-            greet(of_plane(wrapped(lat + i, n_lat), z))
+        for l in range(n_lon):
+            greet(at(wrapped(lat + i, n_lat), l, mem))
             greeted += 1
     for i in range(1, line):
-        for z in range(planes):
-            greet(of_plane(line_start + wrapped(lat - line_start + i, line), z))
+        for l in range(n_lon):
+            greet(at(line_start + wrapped(lat - line_start + i, line), l, mem))
             greeted += 1
     for i in range(1, n_lon):
         greet(at(lat, wrapped(lon + i, n_lon), mem))
@@ -521,20 +521,17 @@
             total = total + scattered[lax.rem(rank + i, plane)]
         gathered[core, pl.ds(start, chunk), :] = total
 
-        def spread(lat_to, z_to, sem):
-            pltpu.make_async_remote_copy(
-                src_ref=piece(gathered.at[core], turn), dst_ref=piece(gathered.at[core], turn),
-                send_sem=ag_send, recv_sem=ag_recv.at[sem],
-                device_id=of_plane(lat_to, z_to), device_id_type=MESH,
-            ).start()
-
-        @pl.when(turn < early)
-        def _():
-            around(functools.partial(spread, sem=0))
-
-        @pl.when(turn >= early)
-        def _():
-            around(functools.partial(spread, sem=1))
+        def spread(lat_to, z_to, far=1):
+            for side in range(1 - far, 2):
+                pltpu.make_async_remote_copy(
+                    src_ref=piece(gathered.at[core], turn), dst_ref=piece(gathered.at[core], turn),
+                    send_sem=ag_send.at[side], recv_sem=ag_recv.at[side],
+                    device_id=at(lat_to, 2 * z_to + (core if side == 0 else 1 - core), mem),
+                    device_id_type=MESH,
+                ).start()
+
+        around(spread)
+        spread(lat, place_z, far=0)
 
     for m in range(n_mem):
         for l in range(n_lon):
@@ -616,30 +613,20 @@
     for store in stores:
         store.start()
 
-    def share(which):
-        start, count = ((0, early), (early, owners - early))[which]
-        span = pl.ds(start * chunk, count * chunk)
-        inside_it = jnp.logical_and(is_owner, jnp.logical_and(turn >= start, turn < start + count))
-        if count > 1:
-            @pl.when(inside_it)
-            def _():
-                passed(halved, (count - 1) * chunk, ag_recv.at[which])
-
-        @pl.when(jnp.logical_not(inside_it))
-        def _():
-            passed(halved, count * chunk, ag_recv.at[which])
-
-        copy = pltpu.make_async_remote_copy(
-            src_ref=gathered.at[core, span], dst_ref=gathered.at[core, span],
-            send_sem=cp_send.at[2 + which], recv_sem=cp_recv.at[2 + which],
-            device_id=at(lat, partner, mem), device_id_type=MESH,
-        )
-        copy.start()
-        return copy, span
-
-    shares = [share(0), share(1)]
-    keep = pltpu.make_async_copy(gathered.at[core], grads.at[core], out_sem.at[2])
-    keep.start()
+    @pl.when(is_owner)
+    def _():
+        passed(halved, (owners - 1) * chunk, ag_recv.at[0])
+
+    @pl.when(jnp.logical_not(is_owner))
+    def _():
+        passed(halved, owners * chunk, ag_recv.at[0])
+
+    def keep(side, sem):
+        return pltpu.make_async_copy(gathered.at[side], grads.at[side], out_sem.at[sem])
+
+    keep(core, 2).start()
+    passed(halved, owners * chunk, ag_recv.at[1])
+    keep(1 - core, 3).start()
 
     for store in stores:
         store.wait()
@@ -675,24 +662,15 @@
     @pl.when(is_owner)
     def _():
         passed(halved, (owners - 1) * chunk, rs_send)
-        passed(scattered, plane - 1, ag_send)
+        passed(scattered, plane - 1, ag_send.at[0])
+        passed(scattered, plane, ag_send.at[1])
 
     @pl.when(jnp.logical_not(is_owner))
     def _():
         passed(halved, owners * chunk, rs_send)
 
-    fetched = []
-    for which, (copy, span) in enumerate(shares):
-        copy.wait()
-        fetched.append(
-            pltpu.make_async_copy(
-                gathered.at[1 - core, span], grads.at[1 - core, span], out_sem.at[3 + which]
-            )
-        )
-        fetched[-1].start()
-    keep.wait()
-    for fetch in fetched:
-        fetch.wait()
+    keep(core, 2).wait()
+    keep(1 - core, 3).wait()
 
 
 def finish(
@@ -790,10 +768,10 @@
             pltpu.VMEM((plane, chunk, 128), F32),
             pltpu.VMEM((2, half, 128), F32),
             dma((8,)),
-            dma((5,)),
+            dma((4,)),
             pltpu.SemaphoreType.REGULAR,
-            dma((4,)),
-            dma((4,)),
+            dma((2,)),
+            dma((2,)),
             dma((3, n_lon)),
             dma((3, n_lon)),
             dma((4,)),
@@ -803,7 +781,7 @@
             dma,
             dma,
             dma,
-            dma,
+            dma((2,)),
             dma((2,)),
         ],
         compiler_params=pltpu.CompilerParams(

time: 37.4 us -> 37.6 us (level)
  no operation moved by 1% of the time
where the time goes in v7:
time: 37.6 us; the launch traced here: 37.4 us
  Pallas kernels  36.8 us (98%)
  between operations  0.64 us (2%)
    pallas_call x1, Pallas kernels, per_device(): pl.pallas_call(functools.partial(kernel, n_lat, n_lon, n_mem), out_shape=...  34.5 us
    pallas_call x1, Pallas kernels, per_device(): pl.pallas_call(finish, out_shape=(*fields, jax.ShapeDtypeStruct((9, 3, mi...  2.25 us

profile of v7, /device:TPU:1, one launch (start us, length us, event | category | flops | bytes accessed | tf_op | source)
XLA Modules:
  0.0 37.4 jit_solution(1029144624917015170)
XLA Ops:
  0.6 34.5 %ocean_step.1 = (f32[2,4,32,512]{3,2,1,0:T(8,128)}, f32[4,32,512]{2,1,0:T(8,128)}, f32[2,384,128]{2,1,0:T(8,128)}) custom-call(f32[2,4,32,512]{3,2,1,0:T(8,128)} %velo_in.1, f32[4,32,512]{2,1,0:T(8,128)} %temp_in.1, s32[32,512]{1,0:T(8,128)} %land_in.1, bf16[2,4,8,128]{3,2,1,0:T(8,128)(2,1)} %target_in.1, bf16[9,3,2,64]{3,2,1,0:T(2,128)(2,1)} %bitcast.2, ...), custom_call_target="tpu_custom_call" | custom-call | tf_op jit(solution)/shard_map/ocean_step/pallas_call | solution.py:732
  35.2 2.2 %finish.1 = (f32[2,4,32,512]{3,2,1,0:T(8,128)}, f32[4,32,512]{2,1,0:T(8,128)}, f32[9,3,2,64]{3,2,1,0:T(2,128)}, f32[2,9,64,64]{3,2,1,0:T(8,128)}, f32[2,9,2,64]{3,2,1,0:T(2,128)}) custom-call(f32[2,4,32,512]{3,2,1,0:T(8,128)} %get-tuple-element.13.velo_in, f32[4,32,512]{2,1,0:T(8,128)} %get-tuple-element.14.temp_in, f32[2,384,128]{2,1,0:T(8,128)} %get-tuple-element.15.halves_in), custom_call_target="tpu_custom_call" | custom-call | tf_op jit(solution)/shard_map/finish/pallas_call | solution.py:792

commit v8 on v7

--- a/solution.py
+++ b/solution.py
@@ -17,28 +17,24 @@
 BF16 = jnp.bfloat16
 MID_ROWS = 9 * HID
 SMALL_ROWS = 72
-GRAD_ROWS = MID_ROWS + 2 * SMALL_ROWS
+GRAD_ROWS = MID_ROWS + SMALL_ROWS
+FIRST_ROWS = 16
 NT = (((1,), (1,)), ((), ()))
 
 
 def chunking(n_lat, planes):
     tiles = -(-GRAD_ROWS // 16)
-    owners = (n_lat // 4 * 3 if n_lat % 4 == 0 else n_lat) * planes
-    return -(-tiles // owners) * 8, owners
-
-
-EARLY = (MID_ROWS + SMALL_ROWS) // 8
-LOW_EARLY, LOW_LATE = (EARLY + 1) // 2, (SMALL_ROWS // 8 + 1) // 2
+    most = (n_lat // 4 * 3 if n_lat % 4 == 0 else n_lat) * planes
+    per = -(-tiles // most)
+    return per * 8, -(-tiles // per)
+
+
+TILES = GRAD_ROWS // 8
+LOW = (TILES + 1) // 2
 
 
 def place(tile):
-    if tile < EARLY:
-        return divmod_half(tile, LOW_EARLY, 0, 0)
-    return divmod_half(tile - EARLY, LOW_LATE, LOW_EARLY, EARLY - LOW_EARLY)
-
-
-def divmod_half(tile, low, base_low, base_high):
-    return (0, 8 * (base_low + tile)) if tile < low else (1, 8 * (base_high + tile - low))
+    return (0, 8 * tile) if tile < LOW else (1, 8 * (tile - LOW))
 
 
 def shift_cols(value, by):
@@ -48,12 +44,13 @@
 def kernel(
     n_lat, n_lon, n_mem,
     velo_in, temp_in, land_in, target_in, first_in, middle_in, last_in,
-    velo_out, temp_out, grads,
+    velo_out, temp_out, grads, small_out,
     velo_new, temp_new, land, target, w_first, w_middle, w_last,
     narrow, tall, staged, send_buf, rx, s0, s1, h2s, g3s, d2s, pred_buf, force_rx, force_up, pad,
     row_send, row_rx, col_send, col_rx, w1_rows, wl_rows, partial, theirs, halved, scattered, gathered,
+    small_part, small_theirs, small_all, small_sum,
     in_sem, out_sem,
-    entered, cp_send, cp_recv, cs_sem, cr_sem, os_sem, or_sem, fs_sem, fr_sem, fl_sem, rs_send, rs_recv, ag_send, ag_recv,
+    entered, cp_send, cp_recv, cs_sem, cr_sem, os_sem, or_sem, fs_sem, fr_sem, fl_sem, rs_send, rs_recv, ag_send, ag_recv, fg_send, fg_recv,
 ):
     lat = lax.axis_index("lat")
     lon = lax.axis_index("lon")
@@ -80,7 +77,7 @@
         return (lat_of - lax.div(lat_of, 4) if n_lat % 4 == 0 else lat_of) * planes + z_of
 
     turn = turn_of(lat, place_z)
-    is_owner = owns(lat)
+    is_owner = jnp.logical_and(owns(lat), turn < owners)
 
     def wrapped(value, size):
         return jnp.where(value >= size, value - size, value)
@@ -123,12 +120,12 @@
     line_start = lax.div(lat, line) * line
     greeted = 0
     for i in range(line, n_lat, line):
-        for l in range(n_lon):
-            greet(at(wrapped(lat + i, n_lat), l, mem))
+        for z in range(planes):
+            greet(of_plane(wrapped(lat + i, n_lat), z))
             greeted += 1
     for i in range(1, line):
-        for l in range(n_lon):
-            greet(at(line_start + wrapped(lat - line_start + i, line), l, mem))
+        for z in range(planes):
+            greet(of_plane(line_start + wrapped(lat - line_start + i, line), z))
             greeted += 1
     for i in range(1, n_lon):
         greet(at(lat, wrapped(lon + i, n_lon), mem))
@@ -448,15 +445,16 @@
         put(at_row, last[32 * a : 32 * a + 24, :])
 
     def core_copy(which):
-        start, size = ((0, split), (split, half - split))[which]
-        return pltpu.make_async_remote_copy(
-            src_ref=partial.at[1 - core, pl.ds(start, size)], dst_ref=theirs.at[pl.ds(start, size)],
+        src, dst = ((partial, theirs), (small_part, small_theirs))[which]
+        return pltpu.make_async_remote_copy(
+            src_ref=src.at[1 - core], dst_ref=dst,
             send_sem=cp_send.at[which], recv_sem=cp_recv.at[which],
             device_id=at(lat, partner, mem), device_id_type=MESH,
         )
 
-    early = 8 * (EARLY - LOW_EARLY) // chunk
-    split = early * chunk
+    for side, used in ((0, 8 * LOW), (1, 8 * (TILES - LOW))):
+        if half > used:
+            partial[side, used:, :] = jnp.zeros((half - used, 128), F32)
     core_copy(0).start()
     if line > 1:
         pl.semaphore_wait(entered, line - 1)
@@ -464,17 +462,14 @@
     def piece(ref, index):
         return ref.at[pl.ds(pl.multiple_of(index * chunk, chunk), chunk)]
 
-    def reduce_rows(which):
-        core_copy(which).wait()
-        start, count = ((0, early), (early, owners - early))[which]
-        span = slice(start * chunk, (start + count) * chunk)
-        halved[span, :] = partial[core, span, :] + theirs[span, :]
+    def reduce_rows():
+        core_copy(0).wait()
+        halved[...] = partial[core] + theirs[...]
 
         def send(lat_to, z_to):
             to = turn_of(lat_to, z_to)
-            wanted = jnp.logical_and(to >= start, to < start + count)
-
-            @pl.when(jnp.logical_and(owns(lat_to), wanted))
+
+            @pl.when(jnp.logical_and(owns(lat_to), to < owners))
             def _():
                 pltpu.make_async_remote_copy(
                     src_ref=piece(halved, to), dst_ref=scattered.at[rank],
@@ -495,19 +490,29 @@
             own.append((taps(products, r, (2, 1, 0)) * (1.0 - h * h)).astype(BF16))
         d1s.append(own)
         if m == 0:
-            reduce_rows(0)
+            reduce_rows()
     first = over_rows(
         lambda r: s0[r + 4 : r + 7].reshape(96, width),
         lambda r: jnp.concatenate([d1s[0][r], d1s[1][r]], axis=0),
     )
-    for a in range(3):
-        at_row = MID_ROWS + SMALL_ROWS + 24 * a
-        put(at_row, first[32 * a : 32 * a + 24, :])
-    used = 8 * (EARLY - LOW_EARLY + SMALL_ROWS // 8 - LOW_LATE)
-    if half > used:
-        partial[1, used:, :] = jnp.zeros((half - used, 128), F32)
+    small_part[...] = jnp.zeros_like(small_part)
+    for k in range(9):
+        for c in range(3):
+            side, row = divmod(3 * k + c, FIRST_ROWS)
+            at_row = 32 * (k // 3) + 8 * (k % 3) + c
+            small_part[side, row : row + 1, :] = first[at_row : at_row + 1, :]
     core_copy(1).start()
-    reduce_rows(1)
+    core_copy(1).wait()
+    small_all[rank] = small_part[core] + small_theirs[...]
+
+    def tell(lat_to, z_to):
+        pltpu.make_async_remote_copy(
+            src_ref=small_all.at[rank], dst_ref=small_all.at[rank],
+            send_sem=fg_send, recv_sem=fg_recv,
+            device_id=of_plane(lat_to, z_to), device_id_type=MESH,
+        ).start()
+
+    around(tell)
 
     def passed(ref, count, sem):
         pltpu.make_async_copy(ref.at[pl.ds(0, count)], ref.at[pl.ds(0, count)], sem).wait()
@@ -521,17 +526,14 @@
             total = total + scattered[lax.rem(rank + i, plane)]
         gathered[core, pl.ds(start, chunk), :] = total
 
-        def spread(lat_to, z_to, far=1):
-            for side in range(1 - far, 2):
-                pltpu.make_async_remote_copy(
-                    src_ref=piece(gathered.at[core], turn), dst_ref=piece(gathered.at[core], turn),
-                    send_sem=ag_send.at[side], recv_sem=ag_recv.at[side],
-                    device_id=at(lat_to, 2 * z_to + (core if side == 0 else 1 - core), mem),
-                    device_id_type=MESH,
-                ).start()
+        def spread(lat_to, z_to):
+            pltpu.make_async_remote_copy(
+                src_ref=piece(gathered.at[core], turn), dst_ref=piece(gathered.at[core], turn),
+                send_sem=ag_send, recv_sem=ag_recv,
+                device_id=of_plane(lat_to, z_to), device_id_type=MESH,
+            ).start()
 
         around(spread)
-        spread(lat, place_z, far=0)
 
     for m in range(n_mem):
         for l in range(n_lon):
@@ -613,20 +615,36 @@
     for store in stores:
         store.start()
 
+    def share(ref, sem):
+        return pltpu.make_async_remote_copy(
+            src_ref=ref.at[core], dst_ref=ref.at[core],
+            send_sem=cp_send.at[sem], recv_sem=cp_recv.at[sem],
+            device_id=at(lat, partner, mem), device_id_type=MESH,
+        )
+
+    def keep(ref, out, side, sem):
+        return pltpu.make_async_copy(ref.at[side], out.at[side], out_sem.at[sem])
+
+    passed(small_all, plane - 1, fg_recv)
+    total = small_all[0]
+    for i in range(1, plane):
+        total = total + small_all[i]
+    small_sum[core] = total
+    share(small_sum, 3).start()
+    keep(small_sum, small_out, core, 4).start()
+
     @pl.when(is_owner)
     def _():
-        passed(halved, (owners - 1) * chunk, ag_recv.at[0])
+        passed(halved, (owners - 1) * chunk, ag_recv)
 
     @pl.when(jnp.logical_not(is_owner))
     def _():
-        passed(halved, owners * chunk, ag_recv.at[0])
-
-    def keep(side, sem):
-        return pltpu.make_async_copy(gathered.at[side], grads.at[side], out_sem.at[sem])
-
-    keep(core, 2).start()
-    passed(halved, owners * chunk, ag_recv.at[1])
-    keep(1 - core, 3).start()
+        passed(halved, owners * chunk, ag_recv)
+
+    share(gathered, 2).start()
+    keep(gathered, grads, core, 2).start()
+    share(small_sum, 3).wait()
+    keep(small_sum, small_out, 1 - core, 5).start()
 
     for store in stores:
         store.wait()
@@ -662,29 +680,35 @@
     @pl.when(is_owner)
     def _():
         passed(halved, (owners - 1) * chunk, rs_send)
-        passed(scattered, plane - 1, ag_send.at[0])
-        passed(scattered, plane, ag_send.at[1])
+        passed(scattered, plane - 1, ag_send)
 
     @pl.when(jnp.logical_not(is_owner))
     def _():
         passed(halved, owners * chunk, rs_send)
 
-    keep(core, 2).wait()
-    keep(1 - core, 3).wait()
+    share(gathered, 2).wait()
+    keep(gathered, grads, 1 - core, 3).start()
+    passed(small_all, plane - 1, fg_send)
+    for ref, out, sem in ((gathered, grads, 2), (small_sum, small_out, 4)):
+        keep(ref, out, core, sem).wait()
+        keep(ref, out, 1 - core, sem + 1).wait()
 
 
 def finish(
-    velo_in, temp_in, halves_in, velo_out, temp_out, first_out, middle_out, last_out,
-    velo, temp, halves, first, middle, last, sems,
+    velo_in, temp_in, halves_in, small_in, velo_out, temp_out, first_out, middle_out, last_out,
+    velo, temp, halves, small, first, middle, last, sems,
 ):
     load = pltpu.make_async_copy(halves_in, halves, sems.at[0])
     load.start()
+    load_small = pltpu.make_async_copy(small_in, small, sems.at[11])
+    load_small.start()
     blocks = [(velo_in.at[c], velo.at[c], velo_out.at[c]) for c in range(2)]
     blocks.append((temp_in, temp, temp_out))
     moves = [pltpu.make_async_copy(b[0], b[1], sems.at[1 + i]) for i, b in enumerate(blocks)]
     for move in moves:
         move.start()
     load.wait()
+    load_small.wait()
 
     def rows_of(start, size, cols):
         side, row = place(start // 8)
@@ -701,8 +725,8 @@
                 at_row = MID_ROWS + (2 - a) * 24 + b * 8 + 4 + 2 * m
                 last[m, k] = rows_of(at_row, 2, cols)
                 for c in range(3):
-                    at_row = MID_ROWS + SMALL_ROWS + a * 24 + b * 8 + c
-                    first[k, c, m : m + 1, :] = rows_of(at_row, 1, cols)
+                    side, row = divmod(3 * k + c, FIRST_ROWS)
+                    first[k, c, m : m + 1, :] = small[side, row : row + 1, cols]
         stores.append(pltpu.make_async_copy(middle.at[m], middle_out.at[m], sems.at[4 + m]))
         stores[-1].start()
     stores.append(pltpu.make_async_copy(first, first_out, sems.at[6]))
@@ -729,11 +753,15 @@
     hbm = pl.BlockSpec(memory_space=pl.ANY)
     dma = pltpu.SemaphoreType.DMA
     fields = [jax.ShapeDtypeStruct(velo.shape, F32), jax.ShapeDtypeStruct(temp.shape, F32)]
-    velo_next, temp_next, grads = pl.pallas_call(
+    velo_next, temp_next, grads, small = pl.pallas_call(
         functools.partial(kernel, n_lat, n_lon, n_mem),
-        out_shape=(*fields, jax.ShapeDtypeStruct((2, half, 128), F32)),
+        out_shape=(
+            *fields,
+            jax.ShapeDtypeStruct((2, half, 128), F32),
+            jax.ShapeDtypeStruct((2, FIRST_ROWS, 128), F32),
+        ),
         in_specs=[hbm] * 7,
-        out_specs=(hbm, hbm, hbm),
+        out_specs=(hbm,) * 4,
         scratch_shapes=[
             pltpu.VMEM(velo.shape, F32),
             pltpu.VMEM(temp.shape, F32),
@@ -767,11 +795,15 @@
             pltpu.VMEM((half, 128), F32),
             pltpu.VMEM((plane, chunk, 128), F32),
             pltpu.VMEM((2, half, 128), F32),
+            pltpu.VMEM((2, FIRST_ROWS, 128), F32),
+            pltpu.VMEM((FIRST_ROWS, 128), F32),
+            pltpu.VMEM((plane, FIRST_ROWS, 128), F32),
+            pltpu.VMEM((2, FIRST_ROWS, 128), F32),
             dma((8,)),
+            dma((6,)),
+            pltpu.SemaphoreType.REGULAR,
             dma((4,)),
-            pltpu.SemaphoreType.REGULAR,
-            dma((2,)),
-            dma((2,)),
+            dma((4,)),
             dma((3, n_lon)),
             dma((3, n_lon)),
             dma((4,)),
@@ -781,8 +813,10 @@
             dma,
             dma,
             dma,
-            dma((2,)),
-            dma((2,)),
+            dma,
+            dma,
+            dma,
+            dma,
         ],
         compiler_params=pltpu.CompilerParams(
             collective_id=0, has_side_effects=True, vmem_limit_bytes=56 * 1024 * 1024
@@ -797,19 +831,20 @@
             jax.ShapeDtypeStruct(w_middle.shape, F32),
             jax.ShapeDtypeStruct(w_last.shape, F32),
         ),
-        in_specs=[hbm] * 3,
+        in_specs=[hbm] * 4,
         out_specs=(hbm,) * 5,
         scratch_shapes=[
             pltpu.VMEM(velo.shape, F32),
             pltpu.VMEM(temp.shape, F32),
             pltpu.VMEM((2, half, 128), F32),
+            pltpu.VMEM((2, FIRST_ROWS, 128), F32),
             pltpu.VMEM((9, 3, mine, HID), F32),
             pltpu.VMEM(w_middle.shape, F32),
             pltpu.VMEM(w_last.shape, F32),
-            dma((11,)),
+            dma((12,)),
         ],
         name="finish",
-    )(velo_next, temp_next, grads)
+    )(velo_next, temp_next, grads, small)
     return (velo_next, temp_next, jnp.transpose(first, (2, 0, 3, 1)), middle, last)
 
 

time: 37.6 us -> 37.6 us (level)
  no operation moved by 1% of the time
where the time goes in v8:
time: 37.6 us; the launch traced here: 37.5 us
  Pallas kernels  36.8 us (98%)
  between operations  0.64 us (2%)
    pallas_call x1, Pallas kernels, per_device(): pl.pallas_call(functools.partial(kernel, n_lat, n_lon, n_mem), out_shape=...  34.6 us
    pallas_call x1, Pallas kernels, per_device(): pl.pallas_call(finish, out_shape=(*fields, jax.ShapeDtypeStruct((9, 3, mi...  2.24 us

profile of v8, /device:TPU:1, one launch (start us, length us, event | category | flops | bytes accessed | tf_op | source)
XLA Modules:
  0.0 37.5 jit_solution(677751489993095321)
XLA Ops:
  0.6 34.6 %ocean_step.1 = (f32[2,4,32,512]{3,2,1,0:T(8,128)}, f32[4,32,512]{2,1,0:T(8,128)}, f32[2,336,128]{2,1,0:T(8,128)}, f32[2,16,128]{2,1,0:T(8,128)}) custom-call(f32[2,4,32,512]{3,2,1,0:T(8,128)} %velo_in.1, f32[4,32,512]{2,1,0:T(8,128)} %temp_in.1, s32[32,512]{1,0:T(8,128)} %land_in.1, bf16[2,4,8,128]{3,2,1,0:T(8,128)(2,1)} %target_in.1, ...), custom_call_target="tpu_custom_call" | custom-call | tf_op jit(solution)/shard_map/ocean_step/pallas_call | solution.py:756
  35.2 2.2 %finish.1 = (f32[2,4,32,512]{3,2,1,0:T(8,128)}, f32[4,32,512]{2,1,0:T(8,128)}, f32[9,3,2,64]{3,2,1,0:T(2,128)}, f32[2,9,64,64]{3,2,1,0:T(8,128)}, f32[2,9,2,64]{3,2,1,0:T(2,128)}) custom-call(f32[2,4,32,512]{3,2,1,0:T(8,128)} %get-tuple-element.14.velo_in, f32[4,32,512]{2,1,0:T(8,128)} %get-tuple-element.15.temp_in, ...), custom_call_target="tpu_custom_call" | custom-call | tf_op jit(solution)/shard_map/finish/pallas_call | solution.py:826

commit v9 on v6

--- a/solution.py
+++ b/solution.py
@@ -355,10 +355,10 @@
         block = s0[r : r + 3].reshape(96, width)
         h = jnp.tanh(jnp.dot(w1, block, preferred_element_type=F32)) * inside(lat * rc - 4 + r)
         for m in range(2):
-            hm = h[m * HID : (m + 1) * HID]
-            s1[m, r, 0:HID] = shift_cols(hm, 1).astype(BF16)
-            s1[m, r, HID : 2 * HID] = hm.astype(BF16)
-            s1[m, r, 2 * HID : 3 * HID] = shift_cols(hm, -1).astype(BF16)
+            hm = h[m * HID : (m + 1) * HID].astype(BF16)
+            s1[m, r, 0:HID] = shift_cols(hm, 1)
+            s1[m, r, HID : 2 * HID] = hm
+            s1[m, r, 2 * HID : 3 * HID] = shift_cols(hm, -1)
 
     def taps(products, r, order):
         return sum(
@@ -417,10 +417,10 @@
         d = jnp.dot(w3t, block, preferred_element_type=F32) * (1.0 - h * h)
         d = d * inside(lat * rc - 1 + r)
         for m in range(2):
-            dm = d[m * HID : (m + 1) * HID]
-            d2s[m, r, 0:HID] = shift_cols(dm, -1).astype(BF16)
-            d2s[m, r, HID : 2 * HID] = dm.astype(BF16)
-            d2s[m, r, 2 * HID : 3 * HID] = shift_cols(dm, 1).astype(BF16)
+            dm = d[m * HID : (m + 1) * HID].astype(BF16)
+            d2s[m, r, 0:HID] = shift_cols(dm, -1)
+            d2s[m, r, HID : 2 * HID] = dm
+            d2s[m, r, 2 * HID : 3 * HID] = shift_cols(dm, 1)
 
     def over_rows(left, right):
         return lax.dot_general(

time: 37.4 us -> 37 us (0.989)
  Pallas kernels: 36.6 us -> 36.2 us
    pallas_call x1, Pallas kernels: 34.3 us -> 34 us  [per_device(): pl.pallas_call(functools.partial(kernel, n_lat, n_lon, n_mem), out_shape=...]
where the time goes in v9:
time: 37 us; the launch traced here: 36.8 us
  Pallas kernels  36.2 us (98%)
  between operations  0.64 us (2%)
    pallas_call x1, Pallas kernels, per_device(): pl.pallas_call(functools.partial(kernel, n_lat, n_lon, n_mem), out_shape=...  34 us
    pallas_call x1, Pallas kernels, per_device(): pl.pallas_call(finish, out_shape=(*fields, jax.ShapeDtypeStruct((9, 3, mi...  2.25 us

profile of v9, /device:TPU:1, one launch (start us, length us, event | category | flops | bytes accessed | tf_op | source)
XLA Modules:
  0.0 36.8 jit_solution(3087157744053363409)
XLA Ops:
  0.6 34.0 %ocean_step.1 = (f32[2,4,32,512]{3,2,1,0:T(8,128)}, f32[4,32,512]{2,1,0:T(8,128)}, f32[2,384,128]{2,1,0:T(8,128)}) custom-call(f32[2,4,32,512]{3,2,1,0:T(8,128)} %velo_in.1, f32[4,32,512]{2,1,0:T(8,128)} %temp_in.1, s32[32,512]{1,0:T(8,128)} %land_in.1, bf16[2,4,8,128]{3,2,1,0:T(8,128)(2,1)} %target_in.1, bf16[9,3,2,64]{3,2,1,0:T(2,128)(2,1)} %bitcast.2, ...), custom_call_target="tpu_custom_call" | custom-call | tf_op jit(solution)/shard_map/ocean_step/pallas_call | solution.py:754
  34.6 2.2 %finish.1 = (f32[2,4,32,512]{3,2,1,0:T(8,128)}, f32[4,32,512]{2,1,0:T(8,128)}, f32[9,3,2,64]{3,2,1,0:T(2,128)}, f32[2,9,64,64]{3,2,1,0:T(8,128)}, f32[2,9,2,64]{3,2,1,0:T(2,128)}) custom-call(f32[2,4,32,512]{3,2,1,0:T(8,128)} %get-tuple-element.13.velo_in, f32[4,32,512]{2,1,0:T(8,128)} %get-tuple-element.14.temp_in, f32[2,384,128]{2,1,0:T(8,128)} %get-tuple-element.15.halves_in), custom_call_target="tpu_custom_call" | custom-call | tf_op jit(solution)/shard_map/finish/pallas_call | solution.py:814

commit v10 on v9

--- a/solution.py
+++ b/solution.py
@@ -342,6 +342,9 @@
     def inside(g):
         return jnp.where(jnp.logical_and(g >= 0, g < nyc), 1.0, 0.0).astype(F32)
 
+    def only_inside(value, r, above):
+        return value if above <= r < above + rc else value * inside(lat * rc - above + r)
+
     def received(x):
         return jnp.concatenate([rx[l, x].astype(F32) for l in range(n_lon)], axis=-1)
 
@@ -353,7 +356,7 @@
 
     for r in range(rc + 8):
         block = s0[r : r + 3].reshape(96, width)
-        h = jnp.tanh(jnp.dot(w1, block, preferred_element_type=F32)) * inside(lat * rc - 4 + r)
+        h = only_inside(jnp.tanh(jnp.dot(w1, block, preferred_element_type=F32)), r, 4)
         for m in range(2):
             hm = h[m * HID : (m + 1) * HID].astype(BF16)
             s1[m, r, 0:HID] = shift_cols(hm, 1)
@@ -370,7 +373,7 @@
             jnp.dot(w2[m], s1[m, x], preferred_element_type=F32) for x in range(rc + 8)
         ]
         for r in range(rc + 6):
-            h = jnp.tanh(taps(products, r, (0, 1, 2))) * inside(lat * rc - 3 + r)
+            h = only_inside(jnp.tanh(taps(products, r, (0, 1, 2))), r, 3)
             h2s[r, m * HID : (m + 1) * HID] = h.astype(BF16)
 
     scale = 2.0 / (2.0 * LEV * nyc * width)
@@ -379,7 +382,7 @@
     for r in range(rc + 4):
         u = [sum(outs[r + a][24 * a + 8 * b : 24 * a + 8 * b + 8] for a in range(3)) for b in range(3)]
         pred = shift_cols(u[0], 1) + u[1] + shift_cols(u[2], -1)
-        g3 = jnp.where(sub >= 4, (pred - received(r + 3)) * scale, 0.0) * inside(lat * rc - 2 + r)
+        g3 = only_inside(jnp.where(sub >= 4, (pred - received(r + 3)) * scale, 0.0), r, 2)
         g3s[r] = jnp.concatenate(
             [shift_cols(g3, -1), g3, shift_cols(g3, 1), jnp.zeros_like(g3)], axis=0
         ).astype(BF16)
@@ -415,7 +418,7 @@
         block = g3s[r : r + 3].reshape(96, width)
         h = h2s[r + 2].astype(F32)
         d = jnp.dot(w3t, block, preferred_element_type=F32) * (1.0 - h * h)
-        d = d * inside(lat * rc - 1 + r)
+        d = only_inside(d, r, 1)
         for m in range(2):
             dm = d[m * HID : (m + 1) * HID].astype(BF16)
             d2s[m, r, 0:HID] = shift_cols(dm, -1)

time: 37 us -> 37 us (level)
  no operation moved by 1% of the time
where the time goes in v10:
time: 37 us; the launch traced here: 36.8 us
  Pallas kernels  36.2 us (98%)
  between operations  0.64 us (2%)
    pallas_call x1, Pallas kernels, per_device(): pl.pallas_call(functools.partial(kernel, n_lat, n_lon, n_mem), out_shape=...  33.9 us
    pallas_call x1, Pallas kernels, per_device(): pl.pallas_call(finish, out_shape=(*fields, jax.ShapeDtypeStruct((9, 3, mi...  2.25 us

profile of v10, /device:TPU:1, one launch (start us, length us, event | category | flops | bytes accessed | tf_op | source)
XLA Modules:
  0.0 36.8 jit_solution(7805854440122488934)
XLA Ops:
  0.6 33.9 %ocean_step.1 = (f32[2,4,32,512]{3,2,1,0:T(8,128)}, f32[4,32,512]{2,1,0:T(8,128)}, f32[2,384,128]{2,1,0:T(8,128)}) custom-call(f32[2,4,32,512]{3,2,1,0:T(8,128)} %velo_in.1, f32[4,32,512]{2,1,0:T(8,128)} %temp_in.1, s32[32,512]{1,0:T(8,128)} %land_in.1, bf16[2,4,8,128]{3,2,1,0:T(8,128)(2,1)} %target_in.1, bf16[9,3,2,64]{3,2,1,0:T(2,128)(2,1)} %bitcast.2, ...), custom_call_target="tpu_custom_call" | custom-call | tf_op jit(solution)/shard_map/ocean_step/pallas_call | solution.py:757
  34.6 2.2 %finish.1 = (f32[2,4,32,512]{3,2,1,0:T(8,128)}, f32[4,32,512]{2,1,0:T(8,128)}, f32[9,3,2,64]{3,2,1,0:T(2,128)}, f32[2,9,64,64]{3,2,1,0:T(8,128)}, f32[2,9,2,64]{3,2,1,0:T(2,128)}) custom-call(f32[2,4,32,512]{3,2,1,0:T(8,128)} %get-tuple-element.13.velo_in, f32[4,32,512]{2,1,0:T(8,128)} %get-tuple-element.14.temp_in, f32[2,384,128]{2,1,0:T(8,128)} %get-tuple-element.15.halves_in), custom_call_target="tpu_custom_call" | custom-call | tf_op jit(solution)/shard_map/finish/pallas_call | solution.py:817
